TPU v7x, 32 devices: a whole 2x2x4 slice. The times are simulated.
32 devices in a mesh: ctx: 4 (over y, core), seq: 4 (over z), tp: 2 (over x).
Axes of the slice: x: 2, y: 2, z: 4, core: 2. Of those that a mesh axis runs over, the one named last changes fastest.
Arguments:
- inputs: bfloat16 [4, 512, 4096], P('seq', 'ctx', 'tp'), may hold values from -6 to 6
- gating: bfloat16 [4, 512, 4096], P('seq', 'ctx', 'tp'), may hold values from -6 to 6
- write_proj: bfloat16 [4, 512, 8, 128], P('seq', 'ctx', 'tp'), may hold values from -6 to 6
- read_proj: bfloat16 [4, 512, 8, 128], P('seq', 'ctx', 'tp'), may hold values from -0.5390625 to 0.5390625
- step_raw: float32 [4, 512, 64], P('seq', 'ctx', 'tp'), may hold values from -2 to 256
- decay_log: float32 [64], P('tp'), may hold values from -11 to -3
- skip_gain: float32 [64], P('tp'), may hold values from 0.5 to 2
- norm_gain: float32 [4096], P('tp'), may hold values from 0.5 to 1.5
- out_weight: bfloat16 [4096, 2048], P('tp', 'ctx'), may hold values from -0.09375 to 0.09375
- residual: bfloat16 [4, 512, 2048], P('seq', 'ctx', 'tp'), may hold values from -32 to 32
- routes: int32 [4, 512, 2], P('seq', 'ctx'), may hold values from 0 to 7, all different within a row; in each aligned block of 128 rows (0 to 127, 128 to 255, ..., all dimensions but the last counted through in order) at most 48 rows name the same one
- route_weight: float32 [4, 512, 2], P('seq', 'ctx'), may hold values from 0.2 to 1
- layer_gain: float32 [2048], P('tp'), may hold values from 0.5 to 1.5
- gate_up_codes: bfloat16 [16, 2, 2048, 768], P(('ctx', 'seq'), None, 'tp'), may hold values from -0.125 to 0.125
- gate_up_scales: float32 [16, 2, 16, 6], P(('ctx', 'seq'), None, 'tp'), may hold values from 0.5 to 2
- down_codes: bfloat16 [16, 768, 2048], P(('ctx', 'seq'), None, 'tp'), may hold values from -0.15625 to 0.15625
- down_scales: float32 [16, 6, 16], P(('ctx', 'seq'), None, 'tp'), may hold values from 0.5 to 2
Outputs:
- mixed: bfloat16 [4, 512, 2048], P('seq', 'ctx', 'tp')
Inputs may be any that keep to these rules, and one draw needn't show every extreme that they name: `routes`: each row names 2 different experts. In each aligned block of 128 rows (the positions of one sequence on one device) no expert is named by more than 48 rows, a bound that some block reaches.
All inputs are finite; a program needn't handle non-finite values.
Results may differ from a plain program's by a relative error of at most 0.033.
Values may be sent and summed in bfloat16 or wider, within the bound.
A program may use at most 64 MiB of HBM per device.

v0:
```python
import jax
import jax.numpy as jnp
from jax import lax
from jax.sharding import PartitionSpec as P

D = 2048
QLEN = 128
QB = 128


EPSILON = 1e-05


def entering(value, axis, combine, identity):
    count, position = (lax.axis_size(axis), lax.axis_index(axis))
    everything = jax.tree.map(
        lambda part, kind: lax.all_gather(part.astype(kind), axis),
        value,
        (jnp.bfloat16, jnp.bfloat16),
    )
    start = jax.tree.map(
        lambda part, zero: jnp.broadcast_to(jnp.asarray(zero, part.dtype), part.shape),
        value,
        identity,
    )

    def hop(k, before):
        reached = k < position
        new = combine(
            before, jax.tree.map(lambda part, own: part[k].astype(own.dtype), everything, value)
        )
        return jax.tree.map(lambda a, b: jnp.where(reached, a, b), new, before)

    return lax.fori_loop(0, count, hop, start)


def expand_scales(scales, width):
    return jnp.repeat(jnp.repeat(scales, width, axis=-2), width, axis=-1)


def join_states(earlier, later):
    return (earlier[0] * later[0], later[0][:, None, None] * earlier[1] + later[1])


def on_device(
    inputs,
    gating,
    write_proj,
    read_proj,
    step_raw,
    decay_log,
    skip_gain,
    norm_gain,
    out_weight,
    residual,
    routes,
    route_weight,
    layer_gain,
    gate_up_codes,
    gate_up_scales,
    down_codes,
    down_scales,
):
    tokens_here = inputs.shape[1]
    heads_here = step_raw.shape[2]
    groups_here = write_proj.shape[2]
    state_width = write_proj.shape[3]
    head_width = inputs.shape[2] // heads_here
    per_group = heads_here // groups_here
    blocks = tokens_here // QLEN
    values = inputs[0].reshape(blocks, QLEN, heads_here, head_width)
    writes = write_proj[0].reshape(blocks, QLEN, groups_here, state_width)
    reads = read_proj[0].reshape(blocks, QLEN, groups_here, state_width)
    stride_size = jax.nn.softplus(step_raw[0]).reshape(blocks, QLEN, heads_here)
    rate = -jnp.exp(decay_log)
    causal_mask = jnp.arange(QLEN)[:, None] >= jnp.arange(QLEN)[None, :]
    lower = causal_mask.astype(jnp.float32)
    cumul = jnp.einsum(
        "ts,bsh->bth", lower, stride_size * rate[None, None, :], precision=lax.Precision.HIGHEST
    )
    scores = jnp.einsum("btgn,bsgn->bgts", reads, writes, preferred_element_type=jnp.float32)
    scores = jnp.repeat(scores, per_group, axis=1)
    cum_heads = jnp.swapaxes(cumul, 1, 2)
    spread = cum_heads[:, :, :, None] - cum_heads[:, :, None, :]
    decay = (
        jnp.where(causal_mask, jnp.exp(jnp.where(causal_mask, spread, 0.0)), 0.0)
        * jnp.swapaxes(stride_size, 1, 2)[:, :, None, :]
    )
    mixing = (scores * decay).astype(jnp.bfloat16)
    local = jnp.einsum("bhts,bshp->bthp", mixing, values, preferred_element_type=jnp.float32)
    final = cumul[:, -1, :]
    coefficient_array = jnp.exp(final[:, None, :] - cumul) * stride_size
    weighted = (values.astype(jnp.float32) * coefficient_array[..., None]).astype(jnp.bfloat16)
    write_heads = jnp.repeat(writes, per_group, axis=2)
    contrib = jnp.einsum(
        "bshp,bshn->bhpn", weighted, write_heads, preferred_element_type=jnp.float32
    )
    keep = jnp.exp(final)
    total_keep = jnp.ones((heads_here,), jnp.float32)
    state_total = jnp.zeros((heads_here, head_width, state_width), jnp.float32)
    state_total = keep[0][:, None, None] * state_total + contrib[0]
    total_keep = total_keep * keep[0]
    identity = (
        jnp.ones((heads_here,), jnp.float32),
        jnp.zeros((heads_here, head_width, state_width), jnp.float32),
    )
    incoming_flow = entering((total_keep, state_total), "ctx", join_states, identity)[1]
    starts = []
    starts.append(incoming_flow)
    starts = jnp.stack(starts)
    read_heads = jnp.repeat(reads, per_group, axis=2).astype(jnp.float32)
    carried = jnp.einsum("bhpn,bthn->bthp", starts, read_heads, precision=lax.Precision.HIGHEST)
    output = (
        local
        + jnp.exp(cumul)[..., None] * carried
        + skip_gain[None, None, :, None] * values.astype(jnp.float32)
    )
    gated = output.reshape(tokens_here, -1) * jax.nn.silu(gating[0].astype(jnp.float32))
    grouped = gated.reshape(tokens_here, groups_here, -1)
    normed = (
        grouped * lax.rsqrt(jnp.mean(grouped * grouped, axis=-1, keepdims=True) + EPSILON)
    ).reshape(tokens_here, -1)
    normed = (normed * norm_gain).astype(jnp.bfloat16)
    partial_value = jnp.dot(
        normed,
        lax.all_gather(out_weight, "ctx", axis=1, tiled=True),
        preferred_element_type=jnp.float32,
    )
    mixer = lax.psum_scatter(
        partial_value.astype(jnp.bfloat16), "tp", scatter_dimension=1, tiled=True
    ).astype(jnp.float32)
    stream = (residual[0].astype(jnp.float32) + mixer).astype(jnp.bfloat16)
    wide = stream.astype(jnp.float32)
    squares = lax.psum(jnp.sum(wide * wide, axis=-1), "tp")
    expert_in = (wide * lax.rsqrt(squares / D + EPSILON)[:, None] * layer_gain).astype(jnp.bfloat16)
    experts = lax.axis_size("ctx") * lax.axis_size("seq") // 2
    capacity = 3 * tokens_here // experts
    feature_width = expert_in.shape[1]
    chosen = routes[0].reshape(-1)
    pair_count = chosen.shape[0]
    ordinal = jnp.arange(pair_count)
    rank = jnp.sum(
        (chosen[:, None] == chosen[None, :]) & (ordinal[None, :] < ordinal[:, None]), axis=1
    )
    target = chosen * capacity + rank
    placed = (jnp.arange(experts * capacity)[:, None] == target[None, :]).reshape(
        experts * capacity, tokens_here, 2
    )
    picker = jnp.any(placed, axis=-1).astype(jnp.bfloat16)
    slots = jnp.dot(picker, expert_in, preferred_element_type=jnp.float32).astype(jnp.bfloat16)
    gate_up = (gate_up_codes[0].astype(jnp.float32) * expand_scales(gate_up_scales[0], QB)).astype(
        jnp.bfloat16
    )
    joined = jnp.concatenate([gate_up[0], gate_up[1]], axis=1)
    down_w = (down_codes[0].astype(jnp.float32) * expand_scales(down_scales[0], QB)).astype(
        jnp.bfloat16
    )
    half_width = down_w.shape[0]
    outgoing = jnp.broadcast_to(
        slots.reshape(experts, 1, capacity, feature_width), (experts, 2, capacity, feature_width)
    )
    outgoing = outgoing.reshape(2 * experts, capacity, feature_width)
    received = lax.all_to_all(outgoing, ("ctx", "seq"), split_axis=0, concat_axis=0, tiled=True)
    sources = received.shape[0]
    items = received.shape[1]
    partial_both = jnp.dot(
        received.reshape(sources * items, feature_width), joined, preferred_element_type=jnp.float32
    )
    shared = lax.psum_scatter(
        partial_both.astype(jnp.bfloat16), "tp", scatter_dimension=0, tiled=True
    ).astype(jnp.float32)
    hidden_part = (jax.nn.silu(shared[:, :half_width]) * shared[:, half_width:]).astype(
        jnp.bfloat16
    )
    hidden = lax.all_gather(hidden_part, "tp", axis=0, tiled=True)
    answered = (
        jnp.dot(hidden, down_w, preferred_element_type=jnp.float32)
        .astype(jnp.bfloat16)
        .reshape(sources, items, feature_width)
    )
    returned = lax.all_to_all(answered, ("ctx", "seq"), split_axis=0, concat_axis=0, tiled=True)
    answers = jnp.sum(
        returned.reshape(experts, 2, capacity, feature_width).astype(jnp.float32), axis=1
    )
    answer_rows = answers.reshape(experts * capacity, feature_width)
    picked = answer_rows[target.reshape(tokens_here, 2)]
    expert_out = jnp.sum(picked * route_weight[0][:, :, None], axis=1)
    return (wide + expert_out).astype(jnp.bfloat16)[None]


def solution(mesh):
    placed = (
        P("seq", "ctx", "tp"),
        P("seq", "ctx", "tp"),
        P("seq", "ctx", "tp", None),
        P("seq", "ctx", "tp", None),
        P("seq", "ctx", "tp"),
        P("tp"),
        P("tp"),
        P("tp"),
        P("tp", "ctx"),
        P("seq", "ctx", "tp"),
        P("seq", "ctx", None),
        P("seq", "ctx", None),
        P("tp"),
        P(("ctx", "seq"), None, "tp", None),
        P(("ctx", "seq"), None, "tp", None),
        P(("ctx", "seq"), None, "tp"),
        P(("ctx", "seq"), None, "tp"),
    )
    return jax.shard_map(
        on_device, mesh=mesh, in_specs=placed, out_specs=P("seq", "ctx", "tp"), check_vma=False
    )
```

profile of v0, /device:TPU:0, one launch (start us, length us, event | category | flops | bytes accessed | tf_op | source)
XLA Modules:
  0.0 294.7 jit_solution(11608897058623656658)
XLA Ops:
  13.8 6.2 %all-gather = bf16[4,1,32]{2,1,0:T(2,128)(2,1)S(1)} all-gather(bf16[1,1,32]{2,1,0:T(2,128)(2,1)} %get-tuple-element.134), channel_id=2, replica_groups=mesh['ctx'=4,'seq'=4,'tp'=2] {'ctx'}, dimensions={0}, use_global_device_ids=true | all-gather | bytes 320 | tf_op jit(solution)/shard_map/all_gather | solution.py:17
  21.4 2.3 copy.103
  24.7 1.8 convolution_bitcast_fusion.1
  26.5 11.8 %all-gather.10.cloned.1.call-done = bf16[128,64,128]{2,1,0:T(8,128)(2,1)} async-done(((bf16[32,64,128]{2,1,0:T(8,128)(2,1)}), bf16[128,64,128]{2,1,0:T(8,128)(2,1)}) %all-gather.10.cloned.1.call-update) | async-done | bytes 2097168 | tf_op jit(solution)/shard_map/all_gather | solution.py:17
  38.3 5.4 %while.14 = (s32[]{:T(128)}, f32[32,64,128]{2,1,0:T(8,128)S(1)}, s32[]{:T(128)}, bf16[4,32]{1,0:T(4,128)(2,1)S(1)}, bf16[4,32,64,128]{3,2,1,0:T(8,128)(2,1)}, /*index=5*/s32[]{:T(128)}, s32[]{:T(128)}) while((s32[]{:T(128)}, f32[32,64,128]{2,1,0:T(8,128)S(1)}, s32[]{:T(128)}, bf16[4,32]{1,0:T(4,128)(2,1)S(1)}, ...), condition=%wide.region_1.2_spmd.clone, body=%wide.region_0.1_spmd.clone.sunk | while | flops 1310756 | bytes 2621865 | solution.py:34
  38.3 1.4 fusion.59
  44.0 4.4 %multiply_reduce_fusion.1 = (f32[128,32]{0,1:T(8,128)S(1)}, f32[1,128,32,64]{1,3,2,0:T(8,128)}) fusion(f32[1,128,32,64]{1,3,2,0:T(8,128)S(1)} %bitcast.166, f32[1,128,32,64]{1,3,2,0:T(8,128)S(1)} %bitcast.165, f32[32]{0:T(128)S(1)} %copy-done.17, f32[1,128,32,64]{1,3,2,0:T(8,128)} %convolution_bitcast_fusion.1, f32[32,64,128]{2,1,0:T(8,128)S(1)} %get-tuple-element.99, ...), kind=kOutput, calls=%fused_computation.39 | convolution fusion | flops 405532672 | bytes 6324352 | tf_op jit(solution)/shard_map/bhpn,bthn->bthp/dot_general | solution.py:112
  50.1 48.0 %all-gather.6.cloned.1.call-done = bf16[2048,2048]{1,0:T(8,128)(2,1)} async-done(((bf16[2048,512]{1,0:T(8,128)(2,1)}), bf16[2048,2048]{1,0:T(8,128)(2,1)}) %all-gather.6.cloned.1.call-update) | async-done | bytes 8388624 | tf_op jit(solution)/shard_map/all_gather | solution.py:126
  98.1 5.9 %convolution_convert_fusion.1 = bf16[128,2048]{1,0:T(8,128)(2,1)} fusion(bf16[2048,2048]{1,0:T(8,128)(2,1)} %all-gather.6.cloned.1.call-done, f32[128,2048]{1,0:T(8,128)S(1)} %bitcast.169, f32[128,2048]{1,0:T(8,128)S(1)} %copy.102, f32[2048]{0:T(1024)S(1)} %copy-done.16, bf16[1,128,2048]{2,1,0:T(8,128)(2,1)} %param.20), kind=kOutput, calls=%fused_computation.13 | convolution fusion | flops 1076363264 | bytes 11542528 | tf_op jit(solution)/shard_map/dot_general | solution.py:124
  104.8 14.0 %reduce-scatter.3.cloned.1.call-done = bf16[128,1024]{1,0:T(8,128)(2,1)} async-done(((bf16[128,2048]{1,0:T(8,128)(2,1)}), bf16[128,1024]{1,0:T(8,128)(2,1)}) %reduce-scatter.3.cloned.1.call-update) | async-done | bytes 262160 | tf_op jit(solution)/shard_map/reduce_scatter | solution.py:129
  119.9 4.9 %psum.7 = f32[128]{0:T(128)S(1)} all-reduce(f32[128]{0:T(128)S(1)} %fusion.21), channel_id=1, replica_groups=mesh['ctx'=4,'seq'=4,'tp'=2] {'tp'}, use_global_device_ids=true, to_apply=%region_8.9 | all-reduce | flops 128 | bytes 1024 | tf_op jit(solution)/shard_map/psum | solution.py:134
  124.8 1.4 convolution_convert_fusion.3
  126.2 1.4 broadcast_in_dim.79
  127.6 5.7 %all-to-all-start = ((bf16[16,48,1024]{2,1,0:T(8,128)(2,1)}), bf16[16,48,1024]{2,1,0:T(8,128)(2,1)}, u32[]{:S(2)}, u32[]{:S(2)}) async-start(bf16[16,48,1024]{2,1,0:T(8,128)(2,1)} %bitcast.30), calls=%async_computation.1 | async-start | bytes 3145728 | tf_op jit(solution)/shard_map/all_to_all | solution.py:163
  133.4 3.2 %copy.108 = bf16[1,2,1024,768]{2,3,1,0:T(8,128)(2,1)S(1)} copy(bf16[1,2,1024,768]{3,2,1,0:T(8,128)(2,1)} %param.32) | data formatting | bytes 6291456 | tf_op args[13]
  139.3 32.1 %all-to-all-done = bf16[16,48,1024]{2,1,0:T(8,128)(2,1)} async-done(((bf16[16,48,1024]{2,1,0:T(8,128)(2,1)}), bf16[16,48,1024]{2,1,0:T(8,128)(2,1)}, u32[]{:S(2)}, u32[]{:S(2)}) %all-to-all-start) | async-done | bytes 1572896 | tf_op jit(solution)/shard_map/all_to_all | solution.py:163
  171.4 6.3 %convolution_convert_fusion = bf16[768,1536]{1,0:T(8,128)(2,1)} fusion(bf16[768,1024]{1,0:T(8,128)(2,1)} %bitcast.31, bf16[1024,768]{0,1:T(8,128)(2,1)S(1)} %get-tuple-element.129, bf16[1024,768]{0,1:T(8,128)(2,1)S(1)} %get-tuple-element.128), kind=kOutput, calls=%fused_computation.6 | convolution fusion | flops 2423390208 | bytes 7077888 | tf_op jit(solution)/shard_map/dot_general | solution.py:166
  178.0 32.5 %reduce-scatter.5.cloned.1.call-done = bf16[384,1536]{1,0:T(8,128)(2,1)} async-done(((bf16[768,1536]{1,0:T(8,128)(2,1)}), bf16[384,1536]{1,0:T(8,128)(2,1)}) %reduce-scatter.5.cloned.1.call-update) | async-done | bytes 1179664 | tf_op jit(solution)/shard_map/reduce_scatter | solution.py:169
  210.5 1.5 convert_element_type.194
  213.3 22.9 %all-gather.8.cloned.1.call-done = bf16[768,768]{1,0:T(8,128)(2,1)} async-done(((bf16[384,768]{1,0:T(8,128)(2,1)}), bf16[768,768]{1,0:T(8,128)(2,1)}) %all-gather.8.cloned.1.call-update) | async-done | bytes 1179664 | tf_op jit(solution)/shard_map/all_gather | solution.py:175
  237.5 2.6 convolution_convert_fusion.2
  240.1 5.8 %all-to-all-start.1 = ((bf16[16,48,1024]{2,1,0:T(8,128)(2,1)}), bf16[16,48,1024]{2,1,0:T(8,128)(2,1)S(1)}, u32[]{:S(2)}, u32[]{:S(2)}) async-start(bf16[16,48,1024]{2,1,0:T(8,128)(2,1)} %bitcast.39), calls=%async_computation.3 | async-start | bytes 3145728 | tf_op jit(solution)/shard_map/all_to_all | solution.py:181
  246.3 37.6 %all-to-all-done.1 = bf16[16,48,1024]{2,1,0:T(8,128)(2,1)S(1)} async-done(((bf16[16,48,1024]{2,1,0:T(8,128)(2,1)}), bf16[16,48,1024]{2,1,0:T(8,128)(2,1)S(1)}, u32[]{:S(2)}, u32[]{:S(2)}) %all-to-all-start.1) | async-done | bytes 1572896 | tf_op jit(solution)/shard_map/all_to_all | solution.py:181
  286.0 1.3 multiply_reduce_fusion
  (108 shorter events, 26.0 us)
Async XLA Ops:
  6.5 31.7 %all-gather.10.cloned.1.call-start = ((), (), s32[]{:S(2)}) async-start(), calls=%async_computation.8 | async-start | bytes 2621440 | tf_op jit(solution)/shard_map/all_gather | solution.py:17
  11.5 2.1 copy-start.2
  12.8 8.6 %copy-start.6 = (bf16[1,128,4,128]{3,2,1,0:T(4,128)(2,1)S(1)}, bf16[1,128,4,128]{3,2,1,0:T(4,128)(2,1)}, u32[]{:S(2)}) copy-start(bf16[1,128,4,128]{3,2,1,0:T(4,128)(2,1)} %param.22) | copy-start | bytes 393220
  12.8 85.3 %all-gather.6.cloned.1.call-start = ((), (), s32[]{:S(2)}) async-start(), calls=%async_computation.4 | async-start | bytes 10485760 | tf_op jit(solution)/shard_map/all_gather | solution.py:126
  13.6 10.1 %copy-start.5 = (bf16[1,128,4,128]{3,2,1,0:T(4,128)(2,1)S(1)}, bf16[1,128,4,128]{3,2,1,0:T(4,128)(2,1)}, u32[]{:S(2)}) copy-start(bf16[1,128,4,128]{3,2,1,0:T(4,128)(2,1)} %param.21) | copy-start | bytes 393220
  13.6 105.2 %reduce-scatter.3.cloned.1.call-start = ((), (), s32[]{:S(2)}) async-start(), calls=%async_computation.5 | async-start | bytes 786432 | tf_op jit(solution)/shard_map/reduce_scatter | solution.py:129
  23.9 14.3 %copy-start.13 = (bf16[4,1,32]{2,0,1:T(4,128)(2,1)S(1)}, bf16[4,1,32]{2,0,1:T(4,128)(2,1)}, u32[]{:S(2)}) copy-start(bf16[4,1,32]{2,0,1:T(4,128)(2,1)} %copy.124) | copy-start | bytes 772
  38.2 5.7 %copy-start.3 = (f32[1,128,2048]{1,2,0:T(8,128)S(1)}, f32[1,128,2048]{1,2,0:T(8,128)}, u32[]{:S(2)}) copy-start(f32[1,128,2048]{1,2,0:T(8,128)} %copy.103) | copy-start | bytes 3145732
  38.2 5.7 %copy-start.7 = (f32[128,32]{0,1:T(8,128)S(1)}, f32[128,32]{0,1:T(8,128)}, u32[]{:S(2)}) copy-start(f32[128,32]{0,1:T(8,128)} %copy.97) | copy-start | bytes 49156
  38.2 5.7 %copy-start.17 = (f32[32]{0:T(128)S(1)}, f32[32]{0:T(128)}, u32[]{:S(2)}) copy-start(f32[32]{0:T(128)} %param.25) | copy-start | bytes 388
  48.4 1.4 copy-start.4
  48.7 49.4 %copy-start.16 = (f32[2048]{0:T(1024)S(1)}, f32[2048]{0:T(1024)}, u32[]{:S(2)}) copy-start(f32[2048]{0:T(1024)} %param.26) | copy-start | bytes 24580
  98.1 5.9 %copy-start.11 = (s32[1,128,2]{1,2,0:T(2,128)S(1)}, s32[1,128,2]{1,2,0:T(2,128)}, u32[]{:S(2)}) copy-start(s32[1,128,2]{1,2,0:T(2,128)} %param.29) | copy-start | bytes 3076
  98.1 20.7 %copy-start = (bf16[1,128,1024]{2,1,0:T(8,128)(2,1)S(1)}, bf16[1,128,1024]{2,1,0:T(8,128)(2,1)}, u32[]{:S(2)}) copy-start(bf16[1,128,1024]{2,1,0:T(8,128)(2,1)} %param.28) | copy-start | bytes 786436
  98.1 26.7 %copy-start.9 = (f32[1024]{0:T(1024)S(1)}, f32[1024]{0:T(1024)}, u32[]{:S(2)}) copy-start(f32[1024]{0:T(1024)} %param.31) | copy-start | bytes 12292
  127.6 43.8 %all-to-all-start = ((bf16[16,48,1024]{2,1,0:T(8,128)(2,1)}), bf16[16,48,1024]{2,1,0:T(8,128)(2,1)}, u32[]{:S(2)}, u32[]{:S(2)}) async-start(bf16[16,48,1024]{2,1,0:T(8,128)(2,1)} %bitcast.30), calls=%async_computation.1 | async-start | bytes 3145728 | tf_op jit(solution)/shard_map/all_to_all | solution.py:163
  133.3 3.3 %copy-start.8 = (f32[1,2,8,6]{2,1,3,0:T(2,128)S(1)}, f32[1,2,8,6]{2,1,3,0:T(2,128)}, u32[]{:S(2)}) copy-start(f32[1,2,8,6]{2,1,3,0:T(2,128)} %param.33) | copy-start | bytes 1156
  133.3 77.2 %reduce-scatter.5.cloned.1.call-start = ((), (), s32[]{:S(2)}) async-start(), calls=%async_computation.6 | async-start | bytes 3538944 | tf_op jit(solution)/shard_map/reduce_scatter | solution.py:169
  177.8 58.4 %all-gather.8.cloned.1.call-start = ((), (), s32[]{:S(2)}) async-start(), calls=%async_computation.7 | async-start | bytes 1769472 | tf_op jit(solution)/shard_map/all_gather | solution.py:175
  213.3 23.8 %copy-start.14 = (bf16[1,768,1024]{2,1,0:T(8,128)(2,1)S(1)}, bf16[1,768,1024]{2,1,0:T(8,128)(2,1)}, u32[]{:S(2)}) copy-start(bf16[1,768,1024]{2,1,0:T(8,128)(2,1)} %param.34) | copy-start | bytes 4718596
  236.2 1.3 copy-start.15
  240.1 6.1 %copy-start.12 = (f32[1,128,2]{1,2,0:T(2,128)S(1)}, f32[1,128,2]{1,2,0:T(2,128)}, u32[]{:S(2)}) copy-start(f32[1,128,2]{1,2,0:T(2,128)} %param.30) | copy-start | bytes 3076
  240.1 43.8 %all-to-all-start.1 = ((bf16[16,48,1024]{2,1,0:T(8,128)(2,1)}), bf16[16,48,1024]{2,1,0:T(8,128)(2,1)S(1)}, u32[]{:S(2)}, u32[]{:S(2)}) async-start(bf16[16,48,1024]{2,1,0:T(8,128)(2,1)} %bitcast.39), calls=%async_computation.3 | async-start | bytes 3145728 | tf_op jit(solution)/shard_map/all_to_all | solution.py:181
  285.4 2.0 copy-start.1
  (1 other events, 1.2 us)
Sparse Core Ops, SparseCore 0:
  12.9 25.2 all-gather.9
  39.8 58.2 all-gather.5
  104.1 14.6 reduce-scatter.2
  177.9 32.5 reduce-scatter.4
  213.4 22.7 all-gather.7
where the time goes:
time: 296 us; the launch traced here: 295 us
  waiting for transfers between devices  200 us (68%)
  matrix products  24.1 us (8%)
  local copies, waits for them, and re-layouts  19.5 us (7%)
  other arithmetic  14.8 us (5%)
  between operations  13.6 us (5%)
  starting transfers between devices  11.8 us (4%)
  blocking collectives  11.2 us (4%)
    all_gather x1, waiting for transfers between devices, on_device(): lax.all_gather(out_weight, 'ctx', axis=1, tiled=True)  48 us
    all_to_all x1, waiting for transfers between devices, on_device(): lax.all_to_all(answered, ('ctx', 'seq'), split_axis=0, concat_axis=0, til...  37.6 us
    reduce_scatter x1, waiting for transfers between devices, on_device(): lax.psum_scatter(partial_both.astype(jnp.bfloat16), 'tp', scatter_dimensi...  32.5 us
    all_to_all x1, waiting for transfers between devices, on_device(): lax.all_to_all(outgoing, ('ctx', 'seq'), split_axis=0, concat_axis=0, til...  32.1 us
    all_gather x1, waiting for transfers between devices, on_device(): hidden = lax.all_gather(hidden_part, 'tp', axis=0, tiled=True)  22.9 us
    reduce_scatter x1, waiting for transfers between devices, on_device(): lax.psum_scatter(partial_value.astype(jnp.bfloat16), 'tp', scatter_dimens...  14 us
    all_gather x1, waiting for transfers between devices, entering(): lax.all_gather(part.astype(kind), axis)  11.8 us
    unnamed x43, local copies, waits for them, and re-layouts  7.45 us
  transfers between devices with their start and end apart: 7, of which 7 were waited for; matrix products, arithmetic and copies ran while one was open for 8% of the time, Pallas kernels for 0%

commit v1 on v0

--- a/solution.py
+++ b/solution.py
@@ -1,7 +1,13 @@
+import functools
+
 import jax
 import jax.numpy as jnp
 from jax import lax
+from jax.experimental import pallas as pl
+from jax.experimental.pallas import tpu as pltpu
 from jax.sharding import PartitionSpec as P
+
+MESH = pl.DeviceIdType.MESH
 
 D = 2048
 QLEN = 128
@@ -34,12 +40,272 @@
     return lax.fori_loop(0, count, hop, start)
 
 
-def expand_scales(scales, width):
-    return jnp.repeat(jnp.repeat(scales, width, axis=-2), width, axis=-1)
-
-
 def join_states(earlier, later):
     return (earlier[0] * later[0], later[0][:, None, None] * earlier[1] + later[1])
+
+
+def flip(index, offset, size):
+    total, bit = 0, 1
+    while bit < size:
+        total = total + bit * ((index // bit + offset // bit) % 2)
+        bit *= 2
+    return total
+
+
+def expert_kernel(
+    sizes,
+    picker_ref,
+    expert_in_ref,
+    gate_up_ref,
+    gate_up_scale_ref,
+    down_ref,
+    down_scale_ref,
+    high_ref,
+    low_ref,
+    stream_ref,
+    out_ref,
+    slots,
+    w_gate_up,
+    w_down,
+    received,
+    partial_out,
+    partial_in,
+    hidden,
+    answers,
+    returned,
+    row_send,
+    row_recv,
+    part_send,
+    part_recv,
+    hid_send,
+    hid_recv,
+    ans_send,
+    ans_recv,
+):
+    n_ctx, n_seq, n_tp = sizes
+    sources = n_ctx * n_seq
+    groups = sources // n_tp
+    capacity, feature_width = slots.shape[1], slots.shape[2]
+    half_width = w_down.shape[0]
+    ctx, seq, tp = lax.axis_index("ctx"), lax.axis_index("seq"), lax.axis_index("tp")
+
+    def at_offset(r):
+        return flip(ctx, r % n_ctx, n_ctx), flip(seq, r // n_ctx, n_seq)
+
+    def row_copy(r):
+        c, s = at_offset(r)
+        return pltpu.make_async_remote_copy(
+            src_ref=slots.at[(c * n_seq + s) // 2],
+            dst_ref=received.at[r],
+            send_sem=row_send.at[r],
+            recv_sem=row_recv.at[r],
+            device_id={"ctx": c, "seq": s},
+            device_id_type=MESH,
+        )
+
+    def part_copy(g, i):
+        peer = lax.rem(tp + i, n_tp)
+        return pltpu.make_async_remote_copy(
+            src_ref=partial_out.at[g * n_tp + peer],
+            dst_ref=partial_in.at[g * (n_tp - 1) + i - 1],
+            send_sem=part_send.at[g * (n_tp - 1) + i - 1],
+            recv_sem=part_recv.at[g * (n_tp - 1) + i - 1],
+            device_id={"tp": peer},
+            device_id_type=MESH,
+        )
+
+    def hid_copy(g, i):
+        peer = lax.rem(tp + i, n_tp)
+        return pltpu.make_async_remote_copy(
+            src_ref=hidden.at[g * n_tp + tp],
+            dst_ref=hidden.at[g * n_tp + tp],
+            send_sem=hid_send.at[g * (n_tp - 1) + i - 1],
+            recv_sem=hid_recv.at[g * (n_tp - 1) + i - 1],
+            device_id={"tp": peer},
+            device_id_type=MESH,
+        )
+
+    def hid_arrival(g, i):
+        origin = lax.rem(tp + n_tp - i, n_tp)
+        return pltpu.make_async_remote_copy(
+            src_ref=hidden.at[g * n_tp + origin],
+            dst_ref=hidden.at[g * n_tp + origin],
+            send_sem=hid_send.at[g * (n_tp - 1) + i - 1],
+            recv_sem=hid_recv.at[g * (n_tp - 1) + i - 1],
+            device_id={"tp": origin},
+            device_id_type=MESH,
+        )
+
+    def ans_copy(r):
+        c, s = at_offset(r)
+        return pltpu.make_async_remote_copy(
+            src_ref=answers.at[r],
+            dst_ref=returned.at[r],
+            send_sem=ans_send.at[r],
+            recv_sem=ans_recv.at[r],
+            device_id={"ctx": c, "seq": s},
+            device_id_type=MESH,
+        )
+
+    barrier = pltpu.get_barrier_semaphore()
+
+    @pl.loop(1, sources)
+    def _(r):
+        c, s = at_offset(r)
+        pl.semaphore_signal(barrier, inc=1, device_id={"ctx": c, "seq": s}, device_id_type=MESH)
+
+    for i in range(1, n_tp):
+        pl.semaphore_signal(
+            barrier, inc=1, device_id={"tp": lax.rem(tp + i, n_tp)}, device_id_type=MESH
+        )
+    experts = slots.shape[0]
+    slots[...] = (
+        jnp.dot(picker_ref[...], expert_in_ref[...], preferred_element_type=jnp.float32)
+        .astype(jnp.bfloat16)
+        .reshape(experts, capacity, feature_width)
+    )
+    pl.semaphore_wait(barrier, sources + n_tp - 2)
+
+    @pl.loop(1, sources)
+    def _(r):
+        row_copy(r).start()
+
+    received[0] = slots[(ctx * n_seq + seq) // 2]
+
+    @pl.loop(0, feature_width // QB)
+    def _(i):
+        rows = pl.ds(pl.multiple_of(i * QB, QB), QB)
+        for kind in range(2):
+            for j in range(half_width // QB):
+                w_gate_up[rows, kind * half_width + j * QB : kind * half_width + (j + 1) * QB] = (
+                    gate_up_ref[kind, rows, j * QB : (j + 1) * QB].astype(jnp.float32)
+                    * gate_up_scale_ref[kind, i, j]
+                ).astype(jnp.bfloat16)
+
+    @pl.loop(0, half_width // QB)
+    def _(i):
+        rows = pl.ds(pl.multiple_of(i * QB, QB), QB)
+        for j in range(feature_width // QB):
+            w_down[rows, j * QB : (j + 1) * QB] = (
+                down_ref[rows, j * QB : (j + 1) * QB].astype(jnp.float32) * down_scale_ref[i, j]
+            ).astype(jnp.bfloat16)
+
+    @pl.loop(0, groups + 2)
+    def _(step):
+        @pl.when(step < groups)
+        def _():
+            g = step
+            for i in range(n_tp):
+                r = g * n_tp + i
+                if i == 0:
+
+                    @pl.when(g > 0)
+                    def _():
+                        row_copy(r).wait_recv()
+                else:
+                    row_copy(r).wait_recv()
+            rows = received[pl.ds(g * n_tp, n_tp)].reshape(n_tp * capacity, feature_width)
+            both = jnp.dot(rows, w_gate_up[...], preferred_element_type=jnp.float32)
+            partial_out[pl.ds(g * n_tp, n_tp)] = both.astype(jnp.bfloat16).reshape(
+                n_tp, capacity, 2 * half_width
+            )
+            for i in range(1, n_tp):
+                part_copy(g, i).start()
+
+        @pl.when((step >= 1) & (step < groups + 1))
+        def _():
+            g = step - 1
+            total = partial_out[g * n_tp + tp].astype(jnp.float32)
+            for i in range(1, n_tp):
+                part_copy(g, i).wait_recv()
+                total = total + partial_in[g * (n_tp - 1) + i - 1].astype(jnp.float32)
+            gate, up = total[:, :half_width], total[:, half_width:]
+            hidden[g * n_tp + tp] = (gate / (1.0 + jnp.exp(-gate)) * up).astype(jnp.bfloat16)
+            for i in range(1, n_tp):
+                hid_copy(g, i).start()
+
+        @pl.when(step >= 2)
+        def _():
+            g = step - 2
+            for i in range(1, n_tp):
+                hid_arrival(g, i).wait_recv()
+            rows = hidden[pl.ds(g * n_tp, n_tp)].reshape(n_tp * capacity, half_width)
+            answer = jnp.dot(rows, w_down[...], preferred_element_type=jnp.float32)
+            answers[pl.ds(g * n_tp, n_tp)] = answer.astype(jnp.bfloat16).reshape(
+                n_tp, capacity, feature_width
+            )
+            for i in range(n_tp):
+                r = g * n_tp + i
+                if i == 0:
+
+                    @pl.when(g > 0)
+                    def _():
+                        ans_copy(r).start()
+                else:
+                    ans_copy(r).start()
+
+    returned[0] = answers[0]
+
+    @pl.loop(1, sources)
+    def _(r):
+        ans_copy(r).wait_recv()
+
+    back = returned[...].reshape(sources * capacity, feature_width)
+    mixed = jnp.dot(high_ref[...], back, preferred_element_type=jnp.float32)
+    mixed = mixed + jnp.dot(low_ref[...], back, preferred_element_type=jnp.float32)
+    out_ref[...] = (stream_ref[...].astype(jnp.float32) + mixed).astype(jnp.bfloat16)
+
+    @pl.loop(1, sources)
+    def _(r):
+        row_copy(r).wait_send()
+        ans_copy(r).wait_send()
+
+    @pl.loop(0, groups)
+    def _(g):
+        for i in range(1, n_tp):
+            part_copy(g, i).wait_send()
+            hid_copy(g, i).wait_send()
+
+
+def expert_layer(picker, expert_in, gate_up, gate_up_scale, down, down_scale, high, low, stream):
+    sizes = tuple(lax.axis_size(axis) for axis in ("ctx", "seq", "tp"))
+    sources, n_tp = sizes[0] * sizes[1], sizes[2]
+    groups = sources // n_tp
+    experts = sources // 2
+    tokens, feature_width = expert_in.shape
+    capacity = picker.shape[0] // experts
+    half_width = down.shape[0]
+    vmem, smem = pl.BlockSpec(memory_space=pltpu.VMEM), pl.BlockSpec(memory_space=pltpu.SMEM)
+    shares = groups * (n_tp - 1)
+    dma = pltpu.SemaphoreType.DMA
+    return pl.pallas_call(
+        functools.partial(expert_kernel, sizes),
+        out_shape=jax.ShapeDtypeStruct((tokens, feature_width), jnp.bfloat16),
+        in_specs=[vmem, vmem, vmem, smem, vmem, smem, vmem, vmem, vmem],
+        out_specs=vmem,
+        scratch_shapes=[
+            pltpu.VMEM((experts, capacity, feature_width), jnp.bfloat16),
+            pltpu.VMEM((feature_width, 2 * half_width), jnp.bfloat16),
+            pltpu.VMEM((half_width, feature_width), jnp.bfloat16),
+            pltpu.VMEM((sources, capacity, feature_width), jnp.bfloat16),
+            pltpu.VMEM((sources, capacity, 2 * half_width), jnp.bfloat16),
+            pltpu.VMEM((shares, capacity, 2 * half_width), jnp.bfloat16),
+            pltpu.VMEM((sources, capacity, half_width), jnp.bfloat16),
+            pltpu.VMEM((sources, capacity, feature_width), jnp.bfloat16),
+            pltpu.VMEM((sources, capacity, feature_width), jnp.bfloat16),
+            dma((sources,)),
+            dma((sources,)),
+            dma((shares,)),
+            dma((shares,)),
+            dma((shares,)),
+            dma((shares,)),
+            dma((sources,)),
+            dma((sources,)),
+        ],
+        compiler_params=pltpu.CompilerParams(
+            collective_id=1, has_side_effects=True, vmem_limit_bytes=56 * 1024 * 1024
+        ),
+    )(picker, expert_in, gate_up, gate_up_scale, down, down_scale, high, low, stream)
 
 
 def on_device(
@@ -133,59 +399,40 @@
     wide = stream.astype(jnp.float32)
     squares = lax.psum(jnp.sum(wide * wide, axis=-1), "tp")
     expert_in = (wide * lax.rsqrt(squares / D + EPSILON)[:, None] * layer_gain).astype(jnp.bfloat16)
-    experts = lax.axis_size("ctx") * lax.axis_size("seq") // 2
-    capacity = 3 * tokens_here // experts
-    feature_width = expert_in.shape[1]
+    n_ctx, n_seq = lax.axis_size("ctx"), lax.axis_size("seq")
+    experts = n_ctx * n_seq // 2
+    capacity = -(-(3 * tokens_here // experts) // 16) * 16
     chosen = routes[0].reshape(-1)
     pair_count = chosen.shape[0]
     ordinal = jnp.arange(pair_count)
     rank = jnp.sum(
         (chosen[:, None] == chosen[None, :]) & (ordinal[None, :] < ordinal[:, None]), axis=1
     )
-    target = chosen * capacity + rank
-    placed = (jnp.arange(experts * capacity)[:, None] == target[None, :]).reshape(
-        experts * capacity, tokens_here, 2
-    )
-    picker = jnp.any(placed, axis=-1).astype(jnp.bfloat16)
-    slots = jnp.dot(picker, expert_in, preferred_element_type=jnp.float32).astype(jnp.bfloat16)
-    gate_up = (gate_up_codes[0].astype(jnp.float32) * expand_scales(gate_up_scales[0], QB)).astype(
-        jnp.bfloat16
-    )
-    joined = jnp.concatenate([gate_up[0], gate_up[1]], axis=1)
-    down_w = (down_codes[0].astype(jnp.float32) * expand_scales(down_scales[0], QB)).astype(
-        jnp.bfloat16
-    )
-    half_width = down_w.shape[0]
-    outgoing = jnp.broadcast_to(
-        slots.reshape(experts, 1, capacity, feature_width), (experts, 2, capacity, feature_width)
-    )
-    outgoing = outgoing.reshape(2 * experts, capacity, feature_width)
-    received = lax.all_to_all(outgoing, ("ctx", "seq"), split_axis=0, concat_axis=0, tiled=True)
-    sources = received.shape[0]
-    items = received.shape[1]
-    partial_both = jnp.dot(
-        received.reshape(sources * items, feature_width), joined, preferred_element_type=jnp.float32
-    )
-    shared = lax.psum_scatter(
-        partial_both.astype(jnp.bfloat16), "tp", scatter_dimension=0, tiled=True
-    ).astype(jnp.float32)
-    hidden_part = (jax.nn.silu(shared[:, :half_width]) * shared[:, half_width:]).astype(
-        jnp.bfloat16
-    )
-    hidden = lax.all_gather(hidden_part, "tp", axis=0, tiled=True)
-    answered = (
-        jnp.dot(hidden, down_w, preferred_element_type=jnp.float32)
-        .astype(jnp.bfloat16)
-        .reshape(sources, items, feature_width)
-    )
-    returned = lax.all_to_all(answered, ("ctx", "seq"), split_axis=0, concat_axis=0, tiled=True)
-    answers = jnp.sum(
-        returned.reshape(experts, 2, capacity, feature_width).astype(jnp.float32), axis=1
-    )
-    answer_rows = answers.reshape(experts * capacity, feature_width)
-    picked = answer_rows[target.reshape(tokens_here, 2)]
-    expert_out = jnp.sum(picked * route_weight[0][:, :, None], axis=1)
-    return (wide + expert_out).astype(jnp.bfloat16)[None]
+    target = (chosen * capacity + rank).reshape(tokens_here, 2)
+    column = jnp.arange(experts * capacity)
+    picker = jnp.any(column[:, None, None] == target[None], axis=-1).astype(jnp.bfloat16)
+    offset = jnp.arange(2 * experts)
+    holder = flip(lax.axis_index("ctx"), offset % n_ctx, n_ctx) * n_seq + flip(
+        lax.axis_index("seq"), offset // n_ctx, n_seq
+    )
+    place = ((holder // 2)[:, None] * capacity + jnp.arange(capacity)[None, :]).reshape(-1)
+    weights = jnp.sum(
+        jnp.where(place[None, :, None] == target[:, None, :], route_weight[0][:, None, :], 0.0),
+        axis=-1,
+    )
+    high = weights.astype(jnp.bfloat16)
+    low = (weights - high.astype(jnp.float32)).astype(jnp.bfloat16)
+    return expert_layer(
+        picker,
+        expert_in,
+        gate_up_codes[0],
+        gate_up_scales[0],
+        down_codes[0],
+        down_scales[0],
+        high,
+        low,
+        stream,
+    )[None]
 
 
 def solution(mesh):

time: 296 us -> 212 us (0.72)
  the two profiles are of different devices: /device:TPU:0 before, /device:TPU:19 now
where the time goes in v1:
time: 212 us; the launch traced here: 210 us
  Pallas kernels  80 us (38%)
  waiting for transfers between devices  68.3 us (32%)
  matrix products  14.1 us (7%)
  local copies, waits for them, and re-layouts  13.4 us (6%)
  between operations  13.4 us (6%)
  other arithmetic  11.2 us (5%)
  blocking collectives  9.49 us (4%)
    pallas_call x1, Pallas kernels, expert_layer(): pl.pallas_call(functools.partial(expert_kernel, sizes), out_shape=jax.Sha...  80 us
    all_gather x1, waiting for transfers between devices, on_device(): lax.all_gather(out_weight, 'ctx', axis=1, tiled=True)  46.8 us
    all_gather x1, waiting for transfers between devices, entering(): lax.all_gather(part.astype(kind), axis)  11.1 us
    reduce_scatter x1, waiting for transfers between devices, on_device(): lax.psum_scatter(partial_value.astype(jnp.bfloat16), 'tp', scatter_dimens...  9.62 us
    unnamed x33, local copies, waits for them, and re-layouts  6.22 us
    dot_general x1, matrix products, on_device(): jnp.dot(normed, lax.all_gather(out_weight, 'ctx', axis=1, tiled=True), pr...  5.98 us
    all_gather x1, blocking collectives, entering(): lax.all_gather(part.astype(kind), axis)  5.7 us
    select_n x4, other arithmetic, hop(): return jax.tree.map(lambda a, b: jnp.where(reached, a, b), new, before)  5.2 us
  transfers between devices with their start and end apart: 3, of which 3 were waited for; matrix products, arithmetic and copies ran while one was open for 11% of the time, Pallas kernels for 0%

profile of v1, /device:TPU:19, one launch (start us, length us, event | category | flops | bytes accessed | tf_op | source)
XLA Modules:
  0.0 210.1 jit_solution(6528906316817626562)
XLA Ops:
  6.5 0.8 copy.77
  9.0 0.9 copy.76
  10.0 1.3 copy.83
  11.5 1.2 fusion.5
  13.8 5.7 %all-gather = bf16[4,1,32]{2,1,0:T(2,128)(2,1)S(1)} all-gather(bf16[1,1,32]{2,1,0:T(2,128)(2,1)} %get-tuple-element.136), channel_id=2, replica_groups=mesh['ctx'=4,'seq'=4,'tp'=2] {'ctx'}, dimensions={0}, use_global_device_ids=true | all-gather | bytes 320 | tf_op jit(solution)/shard_map/all_gather | solution.py:23
  19.7 2.3 %copy.91 = f32[1,128,2048]{1,2,0:T(8,128)} copy(bf16[1,128,2048]{2,1,0:T(8,128)(2,1)} %param.20) | data formatting | bytes 1572864 | tf_op jit(solution)/shard_map/convert_element_type | solution.py:384
  22.0 0.8 copy.72
  24.0 1.8 convolution_bitcast_fusion.1
  25.8 11.1 %all-gather.7.cloned.1.call-done = bf16[128,64,128]{2,1,0:T(8,128)(2,1)} async-done(((bf16[32,64,128]{2,1,0:T(8,128)(2,1)}), bf16[128,64,128]{2,1,0:T(8,128)(2,1)}) %all-gather.7.cloned.1.call-update) | async-done | bytes 2097168 | tf_op jit(solution)/shard_map/all_gather | solution.py:23
  37.0 5.3 %while.14 = (s32[]{:T(128)}, f32[32,64,128]{2,1,0:T(8,128)S(1)}, s32[]{:T(128)}, bf16[4,32]{1,0:T(4,128)(2,1)S(1)}, bf16[4,32,64,128]{3,2,1,0:T(8,128)(2,1)}, /*index=5*/s32[]{:T(128)}, s32[]{:T(128)}) while((s32[]{:T(128)}, f32[32,64,128]{2,1,0:T(8,128)S(1)}, s32[]{:T(128)}, bf16[4,32]{1,0:T(4,128)(2,1)S(1)}, ...), condition=%wide.region_3.4_spmd.clone, body=%wide.region_2.3_spmd.clone.sunk | while | flops 1310756 | bytes 2621865 | solution.py:40
  37.0 1.3 fusion.52
  38.3 1.3 fusion.52
  39.6 1.3 fusion.52
  41.0 1.3 fusion.52
  42.5 4.7 %multiply_reduce_fusion = (f32[128,32]{0,1:T(8,128)S(1)}, f32[1,128,32,64]{1,3,2,0:T(8,128)}) fusion(f32[1,128,32,64]{1,3,2,0:T(8,128)} %bitcast.119, f32[1,128,32,64]{1,3,2,0:T(8,128)S(1)} %bitcast.118, f32[32]{0:T(128)S(1)} %copy-done.12, f32[1,128,32,64]{1,3,2,0:T(8,128)} %convolution_bitcast_fusion.1, f32[32,64,128]{2,1,0:T(8,128)S(1)} %get-tuple-element.99, ...), kind=kOutput, calls=%fused_computation.21 | convolution fusion | flops 405532672 | bytes 6324352 | tf_op jit(solution)/shard_map/bhpn,bthn->bthp/dot_general | solution.py:378
  48.6 1.4 copy.90
  50.0 46.8 %all-gather.5.cloned.1.call-done = bf16[2048,2048]{1,0:T(8,128)(2,1)} async-done(((bf16[2048,512]{1,0:T(8,128)(2,1)}), bf16[2048,2048]{1,0:T(8,128)(2,1)}) %all-gather.5.cloned.1.call-update) | async-done | bytes 8388624 | tf_op jit(solution)/shard_map/all_gather | solution.py:392
  96.9 6.0 %convolution_convert_fusion = bf16[128,2048]{1,0:T(8,128)(2,1)} fusion(bf16[2048,2048]{1,0:T(8,128)(2,1)} %all-gather.5.cloned.1.call-done, f32[128,2048]{1,0:T(8,128)S(1)} %bitcast.122, f32[128,2048]{1,0:T(8,128)} %copy.90, f32[2048]{0:T(1024)S(1)} %copy-done.11, bf16[1,128,2048]{2,1,0:T(8,128)(2,1)S(1)} %copy-done.3), kind=kOutput, calls=%fused_computation.3 | convolution fusion | flops 1076363264 | bytes 11542528 | tf_op jit(solution)/shard_map/dot_general | solution.py:390
  106.5 9.6 %reduce-scatter.2.cloned.1.call-done = bf16[128,1024]{1,0:T(8,128)(2,1)} async-done(((bf16[128,2048]{1,0:T(8,128)(2,1)}), bf16[128,1024]{1,0:T(8,128)(2,1)}) %reduce-scatter.2.cloned.1.call-update) | async-done | bytes 262160 | tf_op jit(solution)/shard_map/reduce_scatter | solution.py:395
  116.1 1.1 fusion.13
  117.3 3.8 %psum.7 = f32[128]{0:T(128)S(1)} all-reduce(f32[128]{0:T(128)S(1)} %get-tuple-element.130), channel_id=1, replica_groups=mesh['ctx'=4,'seq'=4,'tp'=2] {'tp'}, use_global_device_ids=true, to_apply=%region_8.9 | all-reduce | flops 128 | bytes 1024 | tf_op jit(solution)/shard_map/psum | solution.py:400
  121.1 0.8 fusion.15.expert_in_ref
  121.9 80.0 %shard_map.163 = bf16[128,1024]{1,0:T(8,128)(2,1)} custom-call(bf16[384,128]{1,0:T(8,128)(2,1)} %convert_element_type.137.picker_ref, bf16[128,1024]{1,0:T(8,128)(2,1)} %fusion.15.expert_in_ref, bf16[2,1024,768]{2,1,0:T(8,128)(2,1)} %bitcast.115, f32[2,8,6]{2,1,0:T(8,128)} %copy.94.gate_up_scale_ref, bf16[768,1024]{1,0:T(8,128)(2,1)} %bitcast.116, ...), custom_call_target="tpu_custom_call" | custom-call | tf_op jit(solution)/shard_map/pallas_call | solution.py:281
  201.9 1.7 copy.113
  (77 shorter events, 9.5 us)
Async XLA Ops:
  6.5 30.4 %all-gather.7.cloned.1.call-start = ((), (), s32[]{:S(2)}) async-start(), calls=%async_computation.3 | async-start | bytes 2621440 | tf_op jit(solution)/shard_map/all_gather | solution.py:23
  11.5 2.1 copy-start.1
  12.8 6.9 %copy-start.5 = (bf16[1,128,4,128]{3,2,1,0:T(4,128)(2,1)S(1)}, bf16[1,128,4,128]{3,2,1,0:T(4,128)(2,1)}, u32[]{:S(2)}) copy-start(bf16[1,128,4,128]{3,2,1,0:T(4,128)(2,1)} %param.22) | copy-start | bytes 393220
  12.8 84.0 %all-gather.5.cloned.1.call-start = ((), (), s32[]{:S(2)}) async-start(), calls=%async_computation.1 | async-start | bytes 10485760 | tf_op jit(solution)/shard_map/all_gather | solution.py:392
  13.5 9.4 %copy-start.4 = (bf16[1,128,4,128]{3,2,1,0:T(4,128)(2,1)S(1)}, bf16[1,128,4,128]{3,2,1,0:T(4,128)(2,1)}, u32[]{:S(2)}) copy-start(bf16[1,128,4,128]{3,2,1,0:T(4,128)(2,1)} %param.21) | copy-start | bytes 393220
  13.6 102.6 %reduce-scatter.2.cloned.1.call-start = ((), (), s32[]{:S(2)}) async-start(), calls=%async_computation.2 | async-start | bytes 786432 | tf_op jit(solution)/shard_map/reduce_scatter | solution.py:395
  36.9 5.6 %copy-start.12 = (f32[32]{0:T(128)S(1)}, f32[32]{0:T(128)}, u32[]{:S(2)}) copy-start(f32[32]{0:T(128)} %param.25) | copy-start | bytes 388
  47.2 1.4 copy-start.2
  47.6 49.2 %copy-start.3 = (bf16[1,128,2048]{2,1,0:T(8,128)(2,1)S(1)}, bf16[1,128,2048]{2,1,0:T(8,128)(2,1)}, u32[]{:S(2)}) copy-start(bf16[1,128,2048]{2,1,0:T(8,128)(2,1)} %param.20) | copy-start | bytes 1572868
  47.6 49.2 %copy-start.11 = (f32[2048]{0:T(1024)S(1)}, f32[2048]{0:T(1024)}, u32[]{:S(2)}) copy-start(f32[2048]{0:T(1024)} %param.26) | copy-start | bytes 24580
  96.8 7.5 %copy-start.7 = (f32[1,2,8,6]{2,1,3,0:T(2,128)S(1)}, f32[1,2,8,6]{2,1,3,0:T(2,128)}, u32[]{:S(2)}) copy-start(f32[1,2,8,6]{2,1,3,0:T(2,128)} %param.33) | copy-start | bytes 1156
  96.8 8.2 %copy-start.9 = (f32[1,6,8]{2,0,1:T(1,128)S(1)}, f32[1,6,8]{2,0,1:T(1,128)}, u32[]{:S(2)}) copy-start(f32[1,6,8]{2,0,1:T(1,128)} %param.35) | copy-start | bytes 580
  96.8 8.7 %copy-start.10 = (f32[1,128,2]{1,2,0:T(2,128)S(1)}, f32[1,128,2]{1,2,0:T(2,128)}, u32[]{:S(2)}) copy-start(f32[1,128,2]{1,2,0:T(2,128)} %param.30) | copy-start | bytes 3076
  102.8 13.3 %copy-start.6 = (bf16[1,128,1024]{2,1,0:T(8,128)(2,1)S(1)}, bf16[1,128,1024]{2,1,0:T(8,128)(2,1)}, u32[]{:S(2)}) copy-start(bf16[1,128,1024]{2,1,0:T(8,128)(2,1)} %param.28) | copy-start | bytes 786436
  102.8 18.2 %copy-start.8 = (f32[1024]{0:T(1024)S(1)}, f32[1024]{0:T(1024)}, u32[]{:S(2)}) copy-start(f32[1024]{0:T(1024)} %param.31) | copy-start | bytes 12292
  117.3 4.6 %copy-start = (bf16[128,1024]{1,0:T(8,128)(2,1)}, bf16[128,1024]{1,0:T(8,128)(2,1)S(1)}, u32[]{:S(2)}) copy-start(bf16[128,1024]{1,0:T(8,128)(2,1)S(1)} %get-tuple-element.131.stream_ref) | copy-start | bytes 786436
Sparse Core Ops, SparseCore 0:
  12.9 23.9 all-gather.6
  38.5 58.2 all-gather.4
  103.0 13.1 reduce-scatter.1

commit v2 on v1

--- a/solution.py
+++ b/solution.py
@@ -9,39 +9,10 @@
 
 MESH = pl.DeviceIdType.MESH
 
-D = 2048
-QLEN = 128
 QB = 128
 
 
 EPSILON = 1e-05
-
-
-def entering(value, axis, combine, identity):
-    count, position = (lax.axis_size(axis), lax.axis_index(axis))
-    everything = jax.tree.map(
-        lambda part, kind: lax.all_gather(part.astype(kind), axis),
-        value,
-        (jnp.bfloat16, jnp.bfloat16),
-    )
-    start = jax.tree.map(
-        lambda part, zero: jnp.broadcast_to(jnp.asarray(zero, part.dtype), part.shape),
-        value,
-        identity,
-    )
-
-    def hop(k, before):
-        reached = k < position
-        new = combine(
-            before, jax.tree.map(lambda part, own: part[k].astype(own.dtype), everything, value)
-        )
-        return jax.tree.map(lambda a, b: jnp.where(reached, a, b), new, before)
-
-    return lax.fori_loop(0, count, hop, start)
-
-
-def join_states(earlier, later):
-    return (earlier[0] * later[0], later[0][:, None, None] * earlier[1] + later[1])
 
 
 def flip(index, offset, size):
@@ -308,6 +279,350 @@
     )(picker, expert_in, gate_up, gate_up_scale, down, down_scale, high, low, stream)
 
 
+def mixer_kernel(
+    sizes,
+    value_ref,
+    gating_ref,
+    write_ref,
+    read_ref,
+    step_ref,
+    decay_ref,
+    skip_ref,
+    norm_gain_ref,
+    out_weight_ref,
+    residual_ref,
+    layer_gain_ref,
+    stream_ref,
+    expert_in_ref,
+    contrib,
+    state_in,
+    state_out,
+    rows_in,
+    product,
+    mixed_out,
+    mixed_in,
+    square_out,
+    square_in,
+    state_send,
+    state_recv,
+    rows_send,
+    rows_recv,
+    mixed_send,
+    mixed_recv,
+    square_send,
+    square_recv,
+):
+    n_ctx, _, n_tp = sizes
+    ctx, tp = lax.axis_index("ctx"), lax.axis_index("tp")
+    tokens, channels = value_ref.shape
+    heads = step_ref.shape[1]
+    groups, span = rows_in.shape[0], rows_in.shape[3]
+    head_width = channels // heads
+    per_group = heads // groups
+    state_width = write_ref.shape[1] // groups
+    columns, features = out_weight_ref.shape[1], residual_ref.shape[1]
+    owners = features // columns
+    pair = 2 * head_width
+    f32, bf16 = jnp.float32, jnp.bfloat16
+
+    def state_copy(g, target):
+        return pltpu.make_async_remote_copy(
+            src_ref=state_out.at[g],
+            dst_ref=state_in.at[g],
+            send_sem=state_send.at[g],
+            recv_sem=state_recv.at[g],
+            device_id={"ctx": target},
+            device_id_type=MESH,
+        )
+
+    def rows_copy(g, source, slot, offset):
+        return pltpu.make_async_remote_copy(
+            src_ref=rows_in.at[g, source],
+            dst_ref=rows_in.at[g, slot],
+            send_sem=rows_send.at[g * n_ctx + slot],
+            recv_sem=rows_recv.at[g * n_ctx + slot],
+            device_id={"ctx": flip(ctx, offset, n_ctx)},
+            device_id_type=MESH,
+        )
+
+    target_tp = ctx // owners
+
+    def mixed_copy(a, slot):
+        return pltpu.make_async_remote_copy(
+            src_ref=mixed_out.at[a],
+            dst_ref=mixed_in.at[slot],
+            send_sem=mixed_send.at[a],
+            recv_sem=mixed_recv.at[slot],
+            device_id={"ctx": flip(ctx, a, n_ctx), "tp": target_tp},
+            device_id_type=MESH,
+        )
+
+    def square_copy(i):
+        return pltpu.make_async_remote_copy(
+            src_ref=square_out,
+            dst_ref=square_in.at[i - 1],
+            send_sem=square_send.at[i - 1],
+            recv_sem=square_recv.at[i - 1],
+            device_id={"tp": lax.rem(tp + i, n_tp)},
+            device_id_type=MESH,
+        )
+
+    barrier = pltpu.get_barrier_semaphore()
+    for a in range(n_ctx):
+        for i in range(n_tp):
+            if a + i > 0:
+                pl.semaphore_signal(
+                    barrier,
+                    inc=1,
+                    device_id={"ctx": flip(ctx, a, n_ctx), "tp": lax.rem(tp + i, n_tp)},
+                    device_id_type=MESH,
+                )
+
+    step = step_ref[...]
+    stride = jnp.maximum(step, 0.0) + jnp.log1p(jnp.exp(-jnp.abs(step)))
+    at_row = lax.broadcasted_iota(jnp.int32, (tokens, tokens), 0)
+    at_col = lax.broadcasted_iota(jnp.int32, (tokens, tokens), 1)
+    causal = at_row >= at_col
+    cumul = jnp.dot(
+        causal.astype(f32), stride * -jnp.exp(decay_ref[...]), precision=lax.Precision.HIGHEST
+    )
+    cumul_t, stride_t = cumul.T, stride.T
+    final = cumul[tokens - 1 : tokens, :]
+    coefficient = jnp.exp(final - cumul) * stride
+    keep = jnp.exp(final)
+    growth = jnp.exp(cumul)
+    first_half = lax.broadcasted_iota(jnp.int32, (tokens, pair), 1) < head_width
+
+    def widen(table, g):
+        return jnp.concatenate(
+            [
+                jnp.where(first_half, table[:, h : h + 1], table[:, h + 1 : h + 2])
+                for h in range(g * per_group, (g + 1) * per_group, 2)
+            ],
+            axis=1,
+        )
+
+    for g in range(groups):
+        lanes = slice(g * span, (g + 1) * span)
+        weighted = (value_ref[:, lanes].astype(f32) * widen(coefficient, g)).astype(bf16)
+        contrib[g] = lax.dot_general(
+            weighted,
+            write_ref[:, g * state_width : (g + 1) * state_width],
+            (((0,), (0,)), ((), ())),
+            preferred_element_type=f32,
+        )
+
+    pl.semaphore_wait(barrier, n_ctx * n_tp - 1)
+
+    @pl.when(ctx == 0)
+    def _():
+        state_in[...] = jnp.zeros_like(state_in)
+
+    for g in range(groups):
+        lanes = slice(g * span, (g + 1) * span)
+        narrow = slice(g * state_width, (g + 1) * state_width)
+        values = value_ref[:, lanes]
+        scores = lax.dot_general(
+            read_ref[:, narrow],
+            write_ref[:, narrow],
+            (((1,), (1,)), ((), ())),
+            preferred_element_type=f32,
+        )
+        local = []
+        for k in range(per_group // 2):
+            block = values[:, k * pair : (k + 1) * pair]
+            mixing = []
+            for h in (g * per_group + 2 * k, g * per_group + 2 * k + 1):
+                spread = cumul[:, h : h + 1] - cumul_t[h : h + 1, :]
+                decay = jnp.exp(jnp.where(causal, spread, -jnp.inf)) * stride_t[h : h + 1, :]
+                mixing.append((scores * decay).astype(bf16))
+            zero = jnp.zeros_like(block)
+            local.append(
+                jnp.dot(
+                    jnp.concatenate(mixing, axis=1),
+                    jnp.concatenate(
+                        [jnp.where(first_half, block, zero), jnp.where(first_half, zero, block)],
+                        axis=0,
+                    ),
+                    preferred_element_type=f32,
+                )
+            )
+
+        @pl.when(ctx > 0)
+        def _():
+            state_copy(g, ctx - 1).wait_recv()
+
+        @pl.when(ctx < n_ctx - 1)
+        def _():
+            for j in range(per_group):
+                h = g * per_group + j
+                part = slice(j * head_width, (j + 1) * head_width)
+                state_out[g, part, :] = (
+                    state_in[g, part, :].astype(f32) * keep[:, h : h + 1] + contrib[g, part, :]
+                ).astype(bf16)
+            state_copy(g, ctx + 1).start()
+
+        carried = lax.dot_general(
+            read_ref[:, narrow],
+            state_in[g],
+            (((1,), (1,)), ((), ())),
+            preferred_element_type=f32,
+        )
+        skip = jnp.concatenate(
+            [
+                jnp.where(first_half, skip_ref[h], skip_ref[h + 1])
+                for h in range(g * per_group, (g + 1) * per_group, 2)
+            ],
+            axis=1,
+        )
+        output = (
+            jnp.concatenate(local, axis=1)
+            + widen(growth, g) * carried
+            + skip * values.astype(f32)
+        )
+        gate = gating_ref[:, lanes].astype(f32)
+        gated = output * (gate / (1.0 + jnp.exp(-gate)))
+        scale = lax.rsqrt(jnp.mean(gated * gated, axis=1, keepdims=True) + EPSILON)
+        rows_in[g, 0] = (gated * scale * norm_gain_ref[:, lanes]).astype(bf16)
+        for a in range(2, n_ctx, 2):
+            rows_copy(g, 0, a, a).start()
+        rows_copy(g, 0, 1, 1).start()
+
+    def multiply(g):
+        for a in range(1, n_ctx, 2):
+            rows_copy(g, 0, a, a).wait_recv()
+        part = jnp.dot(
+            rows_in[g].reshape(n_ctx * tokens, span),
+            out_weight_ref[g * span : (g + 1) * span, :],
+            preferred_element_type=f32,
+        )
+        if g > 0:
+            part = part + product[...]
+        if g < groups - 1:
+            product[...] = part
+        else:
+            mixed_out[...] = part.astype(bf16).reshape(n_ctx, tokens, columns)
+
+    for g in range(groups):
+        for a in range(2, n_ctx, 2):
+            rows_copy(g, 0, a, a).wait_recv()
+            rows_copy(g, a, a + 1, 1).start()
+        if g > 0:
+            multiply(g - 1)
+    multiply(groups - 1)
+
+    own_slot = lax.rem(ctx, owners) * n_tp + tp
+    for a in range(1, n_ctx):
+        mixed_copy(a, own_slot).start()
+
+    @pl.when(tp == target_tp)
+    def _():
+        mixed_in[own_slot] = mixed_out[0]
+
+    @pl.when(tp != target_tp)
+    def _():
+        mixed_copy(0, own_slot).start()
+
+    squares = jnp.zeros((tokens, 1), f32)
+    for q in range(owners):
+        lanes = slice(q * columns, (q + 1) * columns)
+        total = residual_ref[:, lanes].astype(f32)
+        for i in range(n_tp):
+
+            @pl.when((ctx != tp * owners + q) | (tp != i))
+            def _():
+                mixed_copy(1, q * n_tp + i).wait_recv()
+
+            total = total + mixed_in[q * n_tp + i].astype(f32)
+        total = total.astype(bf16)
+        stream_ref[:, lanes] = total
+        total = total.astype(f32)
+        squares = squares + jnp.sum(total * total, axis=1, keepdims=True)
+    across = jnp.broadcast_to(squares, (tokens, tokens)).T[:8]
+    square_out[...] = across
+    for i in range(1, n_tp):
+        square_copy(i).start()
+    for i in range(1, n_tp):
+        square_copy(i).wait_recv()
+        across = across + square_in[i - 1]
+    squares = jnp.broadcast_to(across[:1], (tokens, tokens)).T[:, :1]
+    scale = lax.rsqrt(squares / (features * n_tp) + EPSILON)
+    expert_in_ref[...] = (stream_ref[...].astype(f32) * scale * layer_gain_ref[...]).astype(bf16)
+
+    for i in range(1, n_tp):
+        square_copy(i).wait_send()
+    for a in range(1, n_ctx):
+        mixed_copy(a, own_slot).wait_send()
+
+    @pl.when(tp != target_tp)
+    def _():
+        mixed_copy(0, own_slot).wait_send()
+
+    for g in range(groups):
+        for a in range(1, n_ctx):
+            rows_copy(g, 0, a, a).wait_send()
+
+    @pl.when(ctx < n_ctx - 1)
+    def _():
+        for g in range(groups):
+            state_copy(g, ctx + 1).wait_send()
+
+
+def mixer_layer(
+    values, gating, writes, reads, step, decay, skip, norm_gain, out_weight, residual, layer_gain
+):
+    sizes = tuple(lax.axis_size(axis) for axis in ("ctx", "seq", "tp"))
+    n_ctx, _, n_tp = sizes
+    tokens, channels = values.shape
+    groups, state_width = writes.shape[1], writes.shape[2]
+    span = channels // groups
+    columns, features = out_weight.shape[1], residual.shape[1]
+    vmem, smem = pl.BlockSpec(memory_space=pltpu.VMEM), pl.BlockSpec(memory_space=pltpu.SMEM)
+    slots = features // columns * n_tp
+    dma = pltpu.SemaphoreType.DMA
+    out = jax.ShapeDtypeStruct((tokens, features), jnp.bfloat16)
+    return pl.pallas_call(
+        functools.partial(mixer_kernel, sizes),
+        out_shape=(out, out),
+        in_specs=[vmem] * 6 + [smem] + [vmem] * 4,
+        out_specs=(vmem, vmem),
+        scratch_shapes=[
+            pltpu.VMEM((groups, span, state_width), jnp.float32),
+            pltpu.VMEM((groups, span, state_width), jnp.bfloat16),
+            pltpu.VMEM((groups, span, state_width), jnp.bfloat16),
+            pltpu.VMEM((groups, n_ctx, tokens, span), jnp.bfloat16),
+            pltpu.VMEM((n_ctx * tokens, columns), jnp.float32),
+            pltpu.VMEM((n_ctx, tokens, columns), jnp.bfloat16),
+            pltpu.VMEM((slots, tokens, columns), jnp.bfloat16),
+            pltpu.VMEM((8, tokens), jnp.float32),
+            pltpu.VMEM((n_tp - 1, 8, tokens), jnp.float32),
+            dma((groups,)),
+            dma((groups,)),
+            dma((groups * n_ctx,)),
+            dma((groups * n_ctx,)),
+            dma((n_ctx,)),
+            dma((slots,)),
+            dma((n_tp - 1,)),
+            dma((n_tp - 1,)),
+        ],
+        compiler_params=pltpu.CompilerParams(
+            collective_id=2, has_side_effects=True, vmem_limit_bytes=48 * 1024 * 1024
+        ),
+    )(
+        values,
+        gating,
+        writes.reshape(tokens, groups * state_width),
+        reads.reshape(tokens, groups * state_width),
+        step,
+        decay[None],
+        skip,
+        norm_gain[None],
+        out_weight,
+        residual,
+        layer_gain[None],
+    )
+
+
 def on_device(
     inputs,
     gating,
@@ -328,77 +643,19 @@
     down_scales,
 ):
     tokens_here = inputs.shape[1]
-    heads_here = step_raw.shape[2]
-    groups_here = write_proj.shape[2]
-    state_width = write_proj.shape[3]
-    head_width = inputs.shape[2] // heads_here
-    per_group = heads_here // groups_here
-    blocks = tokens_here // QLEN
-    values = inputs[0].reshape(blocks, QLEN, heads_here, head_width)
-    writes = write_proj[0].reshape(blocks, QLEN, groups_here, state_width)
-    reads = read_proj[0].reshape(blocks, QLEN, groups_here, state_width)
-    stride_size = jax.nn.softplus(step_raw[0]).reshape(blocks, QLEN, heads_here)
-    rate = -jnp.exp(decay_log)
-    causal_mask = jnp.arange(QLEN)[:, None] >= jnp.arange(QLEN)[None, :]
-    lower = causal_mask.astype(jnp.float32)
-    cumul = jnp.einsum(
-        "ts,bsh->bth", lower, stride_size * rate[None, None, :], precision=lax.Precision.HIGHEST
-    )
-    scores = jnp.einsum("btgn,bsgn->bgts", reads, writes, preferred_element_type=jnp.float32)
-    scores = jnp.repeat(scores, per_group, axis=1)
-    cum_heads = jnp.swapaxes(cumul, 1, 2)
-    spread = cum_heads[:, :, :, None] - cum_heads[:, :, None, :]
-    decay = (
-        jnp.where(causal_mask, jnp.exp(jnp.where(causal_mask, spread, 0.0)), 0.0)
-        * jnp.swapaxes(stride_size, 1, 2)[:, :, None, :]
-    )
-    mixing = (scores * decay).astype(jnp.bfloat16)
-    local = jnp.einsum("bhts,bshp->bthp", mixing, values, preferred_element_type=jnp.float32)
-    final = cumul[:, -1, :]
-    coefficient_array = jnp.exp(final[:, None, :] - cumul) * stride_size
-    weighted = (values.astype(jnp.float32) * coefficient_array[..., None]).astype(jnp.bfloat16)
-    write_heads = jnp.repeat(writes, per_group, axis=2)
-    contrib = jnp.einsum(
-        "bshp,bshn->bhpn", weighted, write_heads, preferred_element_type=jnp.float32
-    )
-    keep = jnp.exp(final)
-    total_keep = jnp.ones((heads_here,), jnp.float32)
-    state_total = jnp.zeros((heads_here, head_width, state_width), jnp.float32)
-    state_total = keep[0][:, None, None] * state_total + contrib[0]
-    total_keep = total_keep * keep[0]
-    identity = (
-        jnp.ones((heads_here,), jnp.float32),
-        jnp.zeros((heads_here, head_width, state_width), jnp.float32),
-    )
-    incoming_flow = entering((total_keep, state_total), "ctx", join_states, identity)[1]
-    starts = []
-    starts.append(incoming_flow)
-    starts = jnp.stack(starts)
-    read_heads = jnp.repeat(reads, per_group, axis=2).astype(jnp.float32)
-    carried = jnp.einsum("bhpn,bthn->bthp", starts, read_heads, precision=lax.Precision.HIGHEST)
-    output = (
-        local
-        + jnp.exp(cumul)[..., None] * carried
-        + skip_gain[None, None, :, None] * values.astype(jnp.float32)
-    )
-    gated = output.reshape(tokens_here, -1) * jax.nn.silu(gating[0].astype(jnp.float32))
-    grouped = gated.reshape(tokens_here, groups_here, -1)
-    normed = (
-        grouped * lax.rsqrt(jnp.mean(grouped * grouped, axis=-1, keepdims=True) + EPSILON)
-    ).reshape(tokens_here, -1)
-    normed = (normed * norm_gain).astype(jnp.bfloat16)
-    partial_value = jnp.dot(
-        normed,
-        lax.all_gather(out_weight, "ctx", axis=1, tiled=True),
-        preferred_element_type=jnp.float32,
-    )
-    mixer = lax.psum_scatter(
-        partial_value.astype(jnp.bfloat16), "tp", scatter_dimension=1, tiled=True
-    ).astype(jnp.float32)
-    stream = (residual[0].astype(jnp.float32) + mixer).astype(jnp.bfloat16)
-    wide = stream.astype(jnp.float32)
-    squares = lax.psum(jnp.sum(wide * wide, axis=-1), "tp")
-    expert_in = (wide * lax.rsqrt(squares / D + EPSILON)[:, None] * layer_gain).astype(jnp.bfloat16)
+    stream, expert_in = mixer_layer(
+        inputs[0],
+        gating[0],
+        write_proj[0],
+        read_proj[0],
+        step_raw[0],
+        decay_log,
+        skip_gain,
+        norm_gain,
+        out_weight,
+        residual[0],
+        layer_gain,
+    )
     n_ctx, n_seq = lax.axis_size("ctx"), lax.axis_size("seq")
     experts = n_ctx * n_seq // 2
     capacity = -(-(3 * tokens_here // experts) // 16) * 16

time: 212 us -> 137 us (0.65)
  waiting for transfers between devices: 68.3 us -> 0 us
  Pallas kernels: 80 us -> 125 us
  matrix products: 14.1 us -> 0 us
  between operations: 13.4 us -> 0.21 us
  blocking collectives: 9.49 us -> 0 us
  other arithmetic: 11.2 us -> 2.71 us
  local copies, waits for them, and re-layouts: 13.4 us -> 8.83 us
    all_gather x2 -> x0, waiting for transfers between devices: 58 us -> none  [the longest x1 46.8 us: on_device(): lax.all_gather(out_weight, 'ctx', axis=1, tiled=True)]
    pallas_call x0 -> x1, Pallas kernels: none -> 43.4 us  [mixer_layer(): pl.pallas_call(functools.partial(mixer_kernel, sizes), out_shape=(out, ou...]
    dot_general x6 -> x0, matrix products: 14.1 us -> none  [the longest x1 5.98 us: on_device(): jnp.dot(normed, lax.all_gather(out_weight, 'ctx', axis=1, tiled=True), pr...]
    reduce_scatter x1 -> x0, waiting for transfers between devices: 9.62 us -> none  [on_device(): lax.psum_scatter(partial_value.astype(jnp.bfloat16), 'tp', scatter_dimens...]
    all_gather x1 -> x0, blocking collectives: 5.7 us -> none  [entering(): lax.all_gather(part.astype(kind), axis)]
    select_n x4 -> x0, other arithmetic: 5.2 us -> none  [hop(): return jax.tree.map(lambda a, b: jnp.where(reached, a, b), new, before)]
    psum x1 -> x0, blocking collectives: 3.79 us -> none  [on_device(): squares = lax.psum(jnp.sum(wide * wide, axis=-1), 'tp')]
    convert_element_type x2 -> x0, local copies, waits for them, and re-layouts: 2.46 us -> none  [the longest x1 2.26 us: on_device(): gating[0].astype(jnp.float32)]
  transfers between devices with their start and end apart: 3 -> 0, of which waited for: 3 -> 0; matrix products, arithmetic and copies ran while one was open for 11% -> 0% of each run, Pallas kernels for 0% -> 0%
where the time goes in v2:
time: 137 us
  Pallas kernels  125 us (91%)
  local copies, waits for them, and re-layouts  8.83 us (6%)
  other arithmetic  2.71 us (2%)
    pallas_call x1, Pallas kernels, expert_layer(): pl.pallas_call(functools.partial(expert_kernel, sizes), out_shape=jax.Sha...  81.7 us
    pallas_call x1, Pallas kernels, mixer_layer(): pl.pallas_call(functools.partial(mixer_kernel, sizes), out_shape=(out, ou...  43.4 us
    unnamed x28, local copies, waits for them, and re-layouts  6.52 us

profile of v2, /device:TPU:19, one launch (start us, length us, event | category | flops | bytes accessed | tf_op | source)
XLA Modules:
  0.0 136.9 jit_solution(5936240948970254812)
XLA Ops:
  0.1 0.1 iota_add_fusion
  0.2 0.1 add.183
  0.3 1.0 copy.28
  1.2 0.1 eq.50
  1.4 0.2 convert_reduce_fusion
  1.6 0.1 reduce_sum.24
  1.7 0.1 copy.32
  1.8 0.9 select_reduce_fusion
  2.7 0.8 subtract_convert_fusion
  3.5 0.1 reduce_sum.23
  3.6 0.1 copy.30
  3.7 0.1 fusion
  3.8 0.7 convert_element_type.16.picker_ref
  4.4 1.0 copy_bitcast_fusion
  5.5 0.8 copy.31
  6.3 0.0 copy-start.2
  6.4 1.0 copy-done.2
  7.4 43.4 %shard_map.163 = (bf16[128,1024]{1,0:T(8,128)(2,1)S(1)}, bf16[128,1024]{1,0:T(8,128)(2,1)S(1)}) custom-call(bf16[128,2048]{1,0:T(8,128)(2,1)S(1)} %bitcast.27, bf16[128,2048]{1,0:T(8,128)(2,1)S(1)} %bitcast.28, bf16[128,512]{1,0:T(8,128)(2,1)S(1)} %get-tuple-element.12.write_ref, bf16[128,512]{1,0:T(8,128)(2,1)S(1)} %get-tuple-element.11.read_ref, ...), custom_call_target="tpu_custom_call" | custom-call | tf_op jit(solution)/shard_map/pallas_call | solution.py:584
  50.8 0.7 copy-done.4
  51.5 0.7 copy-done.5
  52.2 0.7 copy.33.gate_up_scale_ref
  52.8 0.6 copy.40
  53.4 81.7 %shard_map.164 = bf16[128,1024]{1,0:T(8,128)(2,1)} custom-call(bf16[384,128]{1,0:T(8,128)(2,1)} %convert_element_type.16.picker_ref, bf16[128,1024]{1,0:T(8,128)(2,1)} %copy-done.5, bf16[2,1024,768]{2,1,0:T(8,128)(2,1)} %bitcast.34, f32[2,8,6]{2,1,0:T(8,128)} %copy.33.gate_up_scale_ref, bf16[768,1024]{1,0:T(8,128)(2,1)} %bitcast.35, f32[6,8]{1,0:T(8,128)} %bitcast.39, ...), custom_call_target="tpu_custom_call" | custom-call | tf_op jit(solution)/shard_map/pallas_call | solution.py:252
  135.2 1.7 %copy.42 = bf16[1,128,1024]{2,1,0:T(8,128)(2,1)} copy(bf16[1,128,1024]{2,1,0:T(8,128)(2,1)} %bitcast.36) | data formatting | bytes 524288
  (23 shorter events, 0.1 us)
Async XLA Ops:
  0.0 6.3 %copy-start.1 = (bf16[1,128,2048]{2,1,0:T(8,128)(2,1)S(1)}, bf16[1,128,2048]{2,1,0:T(8,128)(2,1)}, u32[]{:S(2)}) copy-start(bf16[1,128,2048]{2,1,0:T(8,128)(2,1)} %param.17) | copy-start | bytes 1572868
  0.0 6.3 %copy-start.8 = (f32[32]{0:T(128)S(1)}, f32[32]{0:T(128)}, u32[]{:S(2)}) copy-start(f32[32]{0:T(128)} %param.22) | copy-start | bytes 388
  0.0 6.3 %copy-start.6 = (f32[2048]{0:T(1024)S(1)}, f32[2048]{0:T(1024)}, u32[]{:S(2)}) copy-start(f32[2048]{0:T(1024)} %param.24) | copy-start | bytes 24580
  0.0 6.3 %copy-start.3 = (bf16[1,128,1024]{2,1,0:T(8,128)(2,1)S(1)}, bf16[1,128,1024]{2,1,0:T(8,128)(2,1)}, u32[]{:S(2)}) copy-start(bf16[1,128,1024]{2,1,0:T(8,128)(2,1)} %param.26) | copy-start | bytes 786436
  0.0 6.3 %copy-start.7 = (f32[1024]{0:T(1024)S(1)}, f32[1024]{0:T(1024)}, u32[]{:S(2)}) copy-start(f32[1024]{0:T(1024)} %param.29) | copy-start | bytes 12292
  0.0 6.3 %copy-start.9 = (f32[32]{0:T(128)S(1)}, f32[32]{0:T(128)}, u32[]{:S(2)}) copy-start(f32[32]{0:T(128)} %skip_ref.1) | copy-start | bytes 388
  0.0 6.3 %copy-start = (bf16[2048,512]{1,0:T(8,128)(2,1)S(1)}, bf16[2048,512]{1,0:T(8,128)(2,1)}, u32[]{:S(2)}) copy-start(bf16[2048,512]{1,0:T(8,128)(2,1)} %out_weight_ref.1) | copy-start | bytes 6291460
  4.4 47.7 %copy-start.10 = (f32[1,2,8,6]{2,1,3,0:T(2,128)S(1)}, f32[1,2,8,6]{2,1,3,0:T(2,128)}, u32[]{:S(2)}) copy-start(f32[1,2,8,6]{2,1,3,0:T(2,128)} %param.31) | copy-start | bytes 1156
  4.4 48.4 %copy-start.11 = (f32[1,6,8]{2,0,1:T(1,128)S(1)}, f32[1,6,8]{2,0,1:T(1,128)}, u32[]{:S(2)}) copy-start(f32[1,6,8]{2,0,1:T(1,128)} %param.33) | copy-start | bytes 580
  6.3 1.0 copy-start.2
  50.8 0.7 copy-start.4
  51.5 0.7 copy-start.5

commit v3 on v2

v3 whole, which is shorter than its diff:
```python
import functools

import jax
import jax.numpy as jnp
from jax import lax
from jax.experimental import pallas as pl
from jax.experimental.pallas import tpu as pltpu
from jax.sharding import PartitionSpec as P

MESH = pl.DeviceIdType.MESH

QB = 128


EPSILON = 1e-05


def flip(index, offset, size):
    total, bit = 0, 1
    while bit < size:
        total = total + bit * ((index // bit + offset // bit) % 2)
        bit *= 2
    return total


def layer_kernel(
    sizes,
    value_ref,
    gating_ref,
    write_ref,
    read_ref,
    step_ref,
    decay_ref,
    skip_ref,
    norm_gain_ref,
    out_weight_hbm,
    residual_ref,
    layer_gain_ref,
    routes_ref,
    route_weight_ref,
    gate_up_hbm,
    gate_up_scale_ref,
    down_hbm,
    down_scale_ref,
    stream_ref,
    mixed_ref,
    out_weight_ref,
    gate_up_ref,
    down_ref,
    fetch_sem,
    contrib,
    state_in,
    state_out,
    rows_in,
    product,
    mixed_out,
    mixed_in,
    square_out,
    square_in,
    state_send,
    state_recv,
    rows_send,
    rows_recv,
    mixed_send,
    mixed_recv,
    square_send,
    square_recv,
    high_slots,
    low_slots,
    high_rows,
    low_rows,
    slots,
    w_gate_up,
    w_down,
    received,
    partial_out,
    partial_in,
    hidden,
    answers,
    returned,
    row_send,
    row_recv,
    part_send,
    part_recv,
    hid_send,
    hid_recv,
    ans_send,
    ans_recv,
):
    n_ctx, n_seq, n_tp = sizes
    ctx, seq, tp = lax.axis_index("ctx"), lax.axis_index("seq"), lax.axis_index("tp")
    tokens, channels = value_ref.shape
    heads = step_ref.shape[0]
    groups, span = rows_in.shape[0], rows_in.shape[3]
    head_width = channels // heads
    per_group = heads // groups
    state_width = write_ref.shape[1] // groups
    columns, features = out_weight_ref.shape[1], residual_ref.shape[1]
    owners = features // columns
    pair = 2 * head_width
    f32, bf16 = jnp.float32, jnp.bfloat16

    def state_copy(g, target):
        return pltpu.make_async_remote_copy(
            src_ref=state_out.at[g],
            dst_ref=state_in.at[g],
            send_sem=state_send.at[g],
            recv_sem=state_recv.at[g],
            device_id={"ctx": target},
            device_id_type=MESH,
        )

    def rows_copy(g, source, slot, offset):
        return pltpu.make_async_remote_copy(
            src_ref=rows_in.at[g, source],
            dst_ref=rows_in.at[g, slot],
            send_sem=rows_send.at[g * n_ctx + slot],
            recv_sem=rows_recv.at[g * n_ctx + slot],
            device_id={"ctx": flip(ctx, offset, n_ctx)},
            device_id_type=MESH,
        )

    target_tp = ctx // owners

    def mixed_copy(a, slot):
        return pltpu.make_async_remote_copy(
            src_ref=mixed_out.at[a],
            dst_ref=mixed_in.at[slot],
            send_sem=mixed_send.at[a],
            recv_sem=mixed_recv.at[slot],
            device_id={"ctx": flip(ctx, a, n_ctx), "tp": target_tp},
            device_id_type=MESH,
        )

    def square_copy(i):
        return pltpu.make_async_remote_copy(
            src_ref=square_out,
            dst_ref=square_in.at[i - 1],
            send_sem=square_send.at[i - 1],
            recv_sem=square_recv.at[i - 1],
            device_id={"tp": lax.rem(tp + i, n_tp)},
            device_id_type=MESH,
        )

    barrier = pltpu.get_barrier_semaphore()
    for a in range(n_ctx):
        for i in range(n_tp):
            if a + i > 0:
                pl.semaphore_signal(
                    barrier,
                    inc=1,
                    device_id={"ctx": flip(ctx, a, n_ctx), "tp": lax.rem(tp + i, n_tp)},
                    device_id_type=MESH,
                )

    @pl.loop(n_ctx, n_ctx * n_seq)
    def _(r):
        pl.semaphore_signal(
            barrier,
            inc=1,
            device_id={"ctx": flip(ctx, r % n_ctx, n_ctx), "seq": flip(seq, r // n_ctx, n_seq)},
            device_id_type=MESH,
        )

    fetches = [
        pltpu.make_async_copy(source, target, fetch_sem.at[k])
        for k, (source, target) in enumerate(
            ((out_weight_hbm, out_weight_ref), (gate_up_hbm, gate_up_ref), (down_hbm, down_ref))
        )
    ]
    for fetch in fetches:
        fetch.start()

    step = step_ref[...]
    stride_t = jnp.maximum(step, 0.0) + jnp.log1p(jnp.exp(-jnp.abs(step)))
    stride = stride_t.T
    at_row = lax.broadcasted_iota(jnp.int32, (tokens, tokens), 0)
    at_col = lax.broadcasted_iota(jnp.int32, (tokens, tokens), 1)
    causal = at_row >= at_col
    cumul = jnp.dot(
        causal.astype(f32), stride * -jnp.exp(decay_ref[...]), precision=lax.Precision.HIGHEST
    )
    cumul_t = cumul.T
    final = cumul[tokens - 1 : tokens, :]
    coefficient = jnp.exp(final - cumul) * stride
    keep = jnp.exp(final)
    growth = jnp.exp(cumul)
    first_half = lax.broadcasted_iota(jnp.int32, (tokens, pair), 1) < head_width

    def widen(table, g):
        return jnp.concatenate(
            [
                jnp.where(first_half, table[:, h : h + 1], table[:, h + 1 : h + 2])
                for h in range(g * per_group, (g + 1) * per_group, 2)
            ],
            axis=1,
        )

    for g in range(groups):
        lanes = slice(g * span, (g + 1) * span)
        weighted = (value_ref[:, lanes].astype(f32) * widen(coefficient, g)).astype(bf16)
        contrib[g] = lax.dot_general(
            weighted,
            write_ref[:, g * state_width : (g + 1) * state_width],
            (((0,), (0,)), ((), ())),
            preferred_element_type=f32,
        )

    pl.semaphore_wait(barrier, n_ctx * (n_tp + n_seq - 1) - 1)

    @pl.when(ctx == 0)
    def _():
        state_in[...] = jnp.zeros_like(state_in)

    for g in range(groups):
        lanes = slice(g * span, (g + 1) * span)
        narrow = slice(g * state_width, (g + 1) * state_width)
        values = value_ref[:, lanes]
        scores = lax.dot_general(
            read_ref[:, narrow],
            write_ref[:, narrow],
            (((1,), (1,)), ((), ())),
            preferred_element_type=f32,
        )
        local = []
        for k in range(per_group // 2):
            block = values[:, k * pair : (k + 1) * pair]
            mixing = []
            for h in (g * per_group + 2 * k, g * per_group + 2 * k + 1):
                spread = cumul[:, h : h + 1] - cumul_t[h : h + 1, :]
                decay = jnp.exp(jnp.where(causal, spread, -jnp.inf)) * stride_t[h : h + 1, :]
                mixing.append((scores * decay).astype(bf16))
            zero = jnp.zeros_like(block)
            local.append(
                jnp.dot(
                    jnp.concatenate(mixing, axis=1),
                    jnp.concatenate(
                        [jnp.where(first_half, block, zero), jnp.where(first_half, zero, block)],
                        axis=0,
                    ),
                    preferred_element_type=f32,
                )
            )

        @pl.when(ctx > 0)
        def _():
            state_copy(g, ctx - 1).wait_recv()

        @pl.when(ctx < n_ctx - 1)
        def _():
            for j in range(per_group):
                h = g * per_group + j
                part = slice(j * head_width, (j + 1) * head_width)
                state_out[g, part, :] = (
                    state_in[g, part, :].astype(f32) * keep[:, h : h + 1] + contrib[g, part, :]
                ).astype(bf16)
            state_copy(g, ctx + 1).start()

        carried = lax.dot_general(
            read_ref[:, narrow],
            state_in[g],
            (((1,), (1,)), ((), ())),
            preferred_element_type=f32,
        )
        skip = jnp.concatenate(
            [
                jnp.where(first_half, skip_ref[h], skip_ref[h + 1])
                for h in range(g * per_group, (g + 1) * per_group, 2)
            ],
            axis=1,
        )
        output = (
            jnp.concatenate(local, axis=1)
            + widen(growth, g) * carried
            + skip * values.astype(f32)
        )
        gate = gating_ref[:, lanes].astype(f32)
        gated = output * (gate / (1.0 + jnp.exp(-gate)))
        scale = lax.rsqrt(jnp.mean(gated * gated, axis=1, keepdims=True) + EPSILON)
        rows_in[g, 0] = (gated * scale * norm_gain_ref[:, lanes]).astype(bf16)
        for a in range(2, n_ctx, 2):
            rows_copy(g, 0, a, a).start()
        rows_copy(g, 0, 1, 1).start()

    experts, capacity, feature_width = slots.shape
    half_width = w_down.shape[0]
    sources = n_ctx * n_seq
    ticks = lax.broadcasted_iota(jnp.int32, (experts, tokens), 0)
    named = [(ticks == routes_ref[k : k + 1, :]).astype(f32) for k in range(2)]
    earlier = jnp.dot(
        (named[0] + named[1]).astype(bf16),
        (at_row < at_col).astype(bf16),
        preferred_element_type=f32,
    )
    place = lax.broadcasted_iota(jnp.int32, (experts * capacity, tokens), 0)
    picker = jnp.zeros((experts * capacity, tokens), f32)
    weights = jnp.zeros((experts * capacity, tokens), f32)
    for k in range(2):
        rank = jnp.sum(named[k] * earlier, axis=0, keepdims=True).astype(jnp.int32)
        hit = place == routes_ref[k : k + 1, :] * capacity + rank
        picker = jnp.where(hit, 1.0, picker)
        weights = jnp.where(hit, route_weight_ref[k : k + 1, :], weights)
    picker = picker.astype(bf16)
    high = weights.astype(bf16)
    low = (weights - high.astype(f32)).astype(bf16)
    high_slots[...] = high.reshape(experts, capacity, tokens)
    low_slots[...] = low.reshape(experts, capacity, tokens)

    @pl.loop(0, sources)
    def _(r):
        holder = flip(ctx, r % n_ctx, n_ctx) * n_seq + flip(seq, r // n_ctx, n_seq)
        high_rows[r] = high_slots[holder // 2]
        low_rows[r] = low_slots[holder // 2]

    fetches[0].wait()

    def multiply(g):
        for a in range(1, n_ctx, 2):
            rows_copy(g, 0, a, a).wait_recv()
        part = jnp.dot(
            rows_in[g].reshape(n_ctx * tokens, span),
            out_weight_ref[g * span : (g + 1) * span, :],
            preferred_element_type=f32,
        )
        if g > 0:
            part = part + product[...]
        if g < groups - 1:
            product[...] = part
        else:
            mixed_out[...] = part.astype(bf16).reshape(n_ctx, tokens, columns)

    for g in range(groups):
        for a in range(2, n_ctx, 2):
            rows_copy(g, 0, a, a).wait_recv()
            rows_copy(g, a, a + 1, 1).start()
        if g > 0:
            multiply(g - 1)
    multiply(groups - 1)

    own_slot = lax.rem(ctx, owners) * n_tp + tp
    for a in range(1, n_ctx):
        mixed_copy(a, own_slot).start()

    @pl.when(tp == target_tp)
    def _():
        mixed_in[own_slot] = mixed_out[0]

    @pl.when(tp != target_tp)
    def _():
        mixed_copy(0, own_slot).start()

    squares = jnp.zeros((tokens, 1), f32)
    for q in range(owners):
        lanes = slice(q * columns, (q + 1) * columns)
        total = residual_ref[:, lanes].astype(f32)
        for i in range(n_tp):

            @pl.when((ctx != tp * owners + q) | (tp != i))
            def _():
                mixed_copy(1, q * n_tp + i).wait_recv()

            total = total + mixed_in[q * n_tp + i].astype(f32)
        total = total.astype(bf16)
        stream_ref[:, lanes] = total
        total = total.astype(f32)
        squares = squares + jnp.sum(total * total, axis=1, keepdims=True)
    across = jnp.broadcast_to(squares, (tokens, tokens)).T[:8]
    square_out[...] = across
    for i in range(1, n_tp):
        square_copy(i).start()
    for i in range(1, n_tp):
        square_copy(i).wait_recv()
        across = across + square_in[i - 1]
    squares = jnp.broadcast_to(across[:1], (tokens, tokens)).T[:, :1]
    scale = lax.rsqrt(squares / (features * n_tp) + EPSILON)
    expert_in = (stream_ref[...].astype(f32) * scale * layer_gain_ref[...]).astype(bf16)
    slots[...] = (
        jnp.dot(picker, expert_in, preferred_element_type=f32)
        .astype(bf16)
        .reshape(experts, capacity, feature_width)
    )

    teams = sources // n_tp

    def at_offset(r):
        return flip(ctx, r % n_ctx, n_ctx), flip(seq, r // n_ctx, n_seq)

    def row_copy(r):
        c, s = at_offset(r)
        return pltpu.make_async_remote_copy(
            src_ref=slots.at[(c * n_seq + s) // 2],
            dst_ref=received.at[r],
            send_sem=row_send.at[r],
            recv_sem=row_recv.at[r],
            device_id={"ctx": c, "seq": s},
            device_id_type=MESH,
        )

    def part_copy(g, i):
        peer = lax.rem(tp + i, n_tp)
        return pltpu.make_async_remote_copy(
            src_ref=partial_out.at[g * n_tp + peer],
            dst_ref=partial_in.at[g * (n_tp - 1) + i - 1],
            send_sem=part_send.at[g * (n_tp - 1) + i - 1],
            recv_sem=part_recv.at[g * (n_tp - 1) + i - 1],
            device_id={"tp": peer},
            device_id_type=MESH,
        )

    def hid_copy(g, i):
        peer = lax.rem(tp + i, n_tp)
        return pltpu.make_async_remote_copy(
            src_ref=hidden.at[g * n_tp + tp],
            dst_ref=hidden.at[g * n_tp + tp],
            send_sem=hid_send.at[g * (n_tp - 1) + i - 1],
            recv_sem=hid_recv.at[g * (n_tp - 1) + i - 1],
            device_id={"tp": peer},
            device_id_type=MESH,
        )

    def hid_arrival(g, i):
        origin = lax.rem(tp + n_tp - i, n_tp)
        return pltpu.make_async_remote_copy(
            src_ref=hidden.at[g * n_tp + origin],
            dst_ref=hidden.at[g * n_tp + origin],
            send_sem=hid_send.at[g * (n_tp - 1) + i - 1],
            recv_sem=hid_recv.at[g * (n_tp - 1) + i - 1],
            device_id={"tp": origin},
            device_id_type=MESH,
        )

    def ans_copy(r):
        c, s = at_offset(r)
        return pltpu.make_async_remote_copy(
            src_ref=answers.at[r],
            dst_ref=returned.at[r],
            send_sem=ans_send.at[r],
            recv_sem=ans_recv.at[r],
            device_id={"ctx": c, "seq": s},
            device_id_type=MESH,
        )

    @pl.loop(1, sources)
    def _(r):
        row_copy(r).start()

    received[0] = slots[(ctx * n_seq + seq) // 2]
    fetches[1].wait()
    fetches[2].wait()

    @pl.loop(0, feature_width // QB)
    def _(i):
        rows = pl.ds(pl.multiple_of(i * QB, QB), QB)
        for kind in range(2):
            for j in range(half_width // QB):
                w_gate_up[rows, kind * half_width + j * QB : kind * half_width + (j + 1) * QB] = (
                    gate_up_ref[kind, rows, j * QB : (j + 1) * QB].astype(jnp.float32)
                    * gate_up_scale_ref[kind, i, j]
                ).astype(jnp.bfloat16)

    @pl.loop(0, half_width // QB)
    def _(i):
        rows = pl.ds(pl.multiple_of(i * QB, QB), QB)
        for j in range(feature_width // QB):
            w_down[rows, j * QB : (j + 1) * QB] = (
                down_ref[rows, j * QB : (j + 1) * QB].astype(jnp.float32) * down_scale_ref[i, j]
            ).astype(jnp.bfloat16)

    @pl.loop(0, teams + 2)
    def _(step):
        @pl.when(step < teams)
        def _():
            g = step
            for i in range(n_tp):
                r = g * n_tp + i
                if i == 0:

                    @pl.when(g > 0)
                    def _():
                        row_copy(r).wait_recv()
                else:
                    row_copy(r).wait_recv()
            rows = received[pl.ds(g * n_tp, n_tp)].reshape(n_tp * capacity, feature_width)
            both = jnp.dot(rows, w_gate_up[...], preferred_element_type=jnp.float32)
            partial_out[pl.ds(g * n_tp, n_tp)] = both.astype(jnp.bfloat16).reshape(
                n_tp, capacity, 2 * half_width
            )
            for i in range(1, n_tp):
                part_copy(g, i).start()

        @pl.when((step >= 1) & (step < teams + 1))
        def _():
            g = step - 1
            total = partial_out[g * n_tp + tp].astype(jnp.float32)
            for i in range(1, n_tp):
                part_copy(g, i).wait_recv()
                total = total + partial_in[g * (n_tp - 1) + i - 1].astype(jnp.float32)
            gate, up = total[:, :half_width], total[:, half_width:]
            hidden[g * n_tp + tp] = (gate / (1.0 + jnp.exp(-gate)) * up).astype(jnp.bfloat16)
            for i in range(1, n_tp):
                hid_copy(g, i).start()

        @pl.when(step >= 2)
        def _():
            g = step - 2
            for i in range(1, n_tp):
                hid_arrival(g, i).wait_recv()
            rows = hidden[pl.ds(g * n_tp, n_tp)].reshape(n_tp * capacity, half_width)
            answer = jnp.dot(rows, w_down[...], preferred_element_type=jnp.float32)
            answers[pl.ds(g * n_tp, n_tp)] = answer.astype(jnp.bfloat16).reshape(
                n_tp, capacity, feature_width
            )
            for i in range(n_tp):
                r = g * n_tp + i
                if i == 0:

                    @pl.when(g > 0)
                    def _():
                        ans_copy(r).start()
                else:
                    ans_copy(r).start()

    returned[0] = answers[0]

    @pl.loop(1, sources)
    def _(r):
        ans_copy(r).wait_recv()

    back = returned[...].reshape(sources * capacity, feature_width)
    contract = (((0,), (0,)), ((), ()))
    mixed = 0.0
    for rows in (high_rows, low_rows):
        mixed = mixed + lax.dot_general(
            rows[...].reshape(sources * capacity, tokens),
            back,
            contract,
            preferred_element_type=f32,
        )
    mixed_ref[...] = mixed

    @pl.loop(1, sources)
    def _(r):
        row_copy(r).wait_send()
        ans_copy(r).wait_send()

    @pl.loop(0, teams)
    def _(g):
        for i in range(1, n_tp):
            part_copy(g, i).wait_send()
            hid_copy(g, i).wait_send()

    for i in range(1, n_tp):
        square_copy(i).wait_send()
    for a in range(1, n_ctx):
        mixed_copy(a, own_slot).wait_send()

    @pl.when(tp != target_tp)
    def _():
        mixed_copy(0, own_slot).wait_send()

    for g in range(groups):
        for a in range(1, n_ctx):
            rows_copy(g, 0, a, a).wait_send()

    @pl.when(ctx < n_ctx - 1)
    def _():
        for g in range(groups):
            state_copy(g, ctx + 1).wait_send()


def both_layers(
    values,
    gating,
    writes,
    reads,
    step,
    decay,
    skip,
    norm_gain,
    out_weight,
    residual,
    layer_gain,
    routes,
    route_weight,
    gate_up,
    gate_up_scale,
    down,
    down_scale,
):
    sizes = tuple(lax.axis_size(axis) for axis in ("ctx", "seq", "tp"))
    n_ctx, n_seq, n_tp = sizes
    tokens, channels = values.shape
    groups, state_width = writes.shape[1], writes.shape[2]
    span = channels // groups
    columns, features = out_weight.shape[1], residual.shape[1]
    sources = n_ctx * n_seq
    experts = sources // 2
    capacity = -(-(3 * tokens // experts) // 16) * 16
    half_width = down.shape[0]
    shares = sources // n_tp * (n_tp - 1)
    slots = features // columns * n_tp
    dma = pltpu.SemaphoreType.DMA
    vmem, smem = pl.BlockSpec(memory_space=pltpu.VMEM), pl.BlockSpec(memory_space=pltpu.SMEM)
    hbm = pl.BlockSpec(memory_space=pl.ANY)

    def wide(*shape):
        return pltpu.VMEM(shape, jnp.float32)

    def half(*shape):
        return pltpu.VMEM(shape, jnp.bfloat16)

    stream, mixed = pl.pallas_call(
        functools.partial(layer_kernel, sizes),
        out_shape=(
            jax.ShapeDtypeStruct((tokens, features), jnp.bfloat16),
            jax.ShapeDtypeStruct((tokens, features), jnp.float32),
        ),
        in_specs=[vmem] * 6
        + [smem, vmem, hbm, vmem, vmem, vmem, vmem]
        + [hbm, smem, hbm, smem],
        out_specs=(vmem, vmem),
        scratch_shapes=[
            half(*out_weight.shape),
            half(*gate_up.shape),
            half(*down.shape),
            dma((3,)),
            wide(groups, span, state_width),
            half(groups, span, state_width),
            half(groups, span, state_width),
            half(groups, n_ctx, tokens, span),
            wide(n_ctx * tokens, columns),
            half(n_ctx, tokens, columns),
            half(slots, tokens, columns),
            wide(8, tokens),
            wide(n_tp - 1, 8, tokens),
            dma((groups,)),
            dma((groups,)),
            dma((groups * n_ctx,)),
            dma((groups * n_ctx,)),
            dma((n_ctx,)),
            dma((slots,)),
            dma((n_tp - 1,)),
            dma((n_tp - 1,)),
            half(experts, capacity, tokens),
            half(experts, capacity, tokens),
            half(sources, capacity, tokens),
            half(sources, capacity, tokens),
            half(experts, capacity, features),
            half(features, 2 * half_width),
            half(half_width, features),
            half(sources, capacity, features),
            half(sources, capacity, 2 * half_width),
            half(shares, capacity, 2 * half_width),
            half(sources, capacity, half_width),
            half(sources, capacity, features),
            half(sources, capacity, features),
            dma((sources,)),
            dma((sources,)),
            dma((shares,)),
            dma((shares,)),
            dma((shares,)),
            dma((shares,)),
            dma((sources,)),
            dma((sources,)),
        ],
        compiler_params=pltpu.CompilerParams(
            collective_id=1, has_side_effects=True, vmem_limit_bytes=60 * 1024 * 1024
        ),
    )(
        values,
        gating,
        writes.reshape(tokens, groups * state_width),
        reads.reshape(tokens, groups * state_width),
        step.T,
        decay[None],
        skip,
        norm_gain[None],
        out_weight,
        residual,
        layer_gain[None],
        routes.T,
        route_weight.T,
        gate_up,
        gate_up_scale,
        down,
        down_scale,
    )
    return (stream.astype(jnp.float32) + mixed).astype(jnp.bfloat16)


def on_device(
    inputs,
    gating,
    write_proj,
    read_proj,
    step_raw,
    decay_log,
    skip_gain,
    norm_gain,
    out_weight,
    residual,
    routes,
    route_weight,
    layer_gain,
    gate_up_codes,
    gate_up_scales,
    down_codes,
    down_scales,
):
    return both_layers(
        inputs[0],
        gating[0],
        write_proj[0],
        read_proj[0],
        step_raw[0],
        decay_log,
        skip_gain,
        norm_gain,
        out_weight,
        residual[0],
        layer_gain,
        routes[0],
        route_weight[0],
        gate_up_codes[0],
        gate_up_scales[0],
        down_codes[0],
        down_scales[0],
    )[None]


def solution(mesh):
    placed = (
        P("seq", "ctx", "tp"),
        P("seq", "ctx", "tp"),
        P("seq", "ctx", "tp", None),
        P("seq", "ctx", "tp", None),
        P("seq", "ctx", "tp"),
        P("tp"),
        P("tp"),
        P("tp"),
        P("tp", "ctx"),
        P("seq", "ctx", "tp"),
        P("seq", "ctx", None),
        P("seq", "ctx", None),
        P("tp"),
        P(("ctx", "seq"), None, "tp", None),
        P(("ctx", "seq"), None, "tp", None),
        P(("ctx", "seq"), None, "tp"),
        P(("ctx", "seq"), None, "tp"),
    )
    return jax.shard_map(
        on_device, mesh=mesh, in_specs=placed, out_specs=P("seq", "ctx", "tp"), check_vma=False
    )
```

time: 137 us -> 127 us (0.927)
  local copies, waits for them, and re-layouts: 8.83 us -> 4.32 us
  Pallas kernels: 125 us -> 121 us
    unnamed x28 -> x1, local copies, waits for them, and re-layouts: 6.52 us -> 1.27 us
    pallas_call x2 -> x1, Pallas kernels: 125 us -> 121 us  [both_layers(): pl.pallas_call(functools.partial(layer_kernel, sizes), out_shape=(jax.Sha...]
    broadcast_in_dim x0 -> x1, other arithmetic: none -> 1.87 us  [on_device(): both_layers(inputs[0], gating[0], write_proj[0], read_proj[0], step_raw[0...]
    convert_element_type x2 -> x0, other arithmetic: 1.46 us -> none  [the longest x1 0.79 us: on_device(): low = (weights - high.astype(jnp.float32)).astype(jnp.bfloat16)]
where the time goes in v3:
time: 127 us
  Pallas kernels  121 us (95%)
  local copies, waits for them, and re-layouts  4.32 us (3%)
  other arithmetic  1.87 us (1%)
    pallas_call x1, Pallas kernels, both_layers(): pl.pallas_call(functools.partial(layer_kernel, sizes), out_shape=(jax.Sha...  121 us

profile of v3, /device:TPU:19, one launch (start us, length us, event | category | flops | bytes accessed | tf_op | source)
XLA Modules:
  0.0 126.9 jit_solution(6305355803366462941)
XLA Ops:
  0.0 1.3 %copy.25 = f32[1,6,8]{2,1,0:T(8,128)} copy(f32[1,6,8]{2,0,1:T(1,128)} %param.33) | data formatting | bytes 384
  1.3 1.4 %copy.18.gate_up_scale_ref = f32[2,8,6]{2,1,0:T(8,128)} copy(f32[2,8,6]{1,0,2:T(2,128)} %bitcast.41) | data formatting | bytes 768 | tf_op jit(solution)/shard_map/squeeze | solution.py:725
  2.6 1.7 %copy_bitcast_fusion = (bf16[128,512]{1,0:T(8,128)(2,1)}, bf16[128,512]{1,0:T(8,128)(2,1)}) fusion(bf16[16,8,4,128]{3,2,1,0:T(4,128)(2,1)} %bitcast.36, bf16[16,8,4,128]{3,2,1,0:T(4,128)(2,1)} %bitcast.37), kind=kLoop, calls=%fused_computation.2 | loop fusion | bytes 524288 | tf_op jit(solution)/shard_map/reshape;squeeze | solution.py:673
  4.3 120.7 %shard_map.163 = (bf16[128,1024]{1,0:T(8,128)(2,1)}, f32[128,1024]{1,0:T(8,128)}) custom-call(bf16[128,2048]{1,0:T(8,128)(2,1)} %bitcast.33, bf16[128,2048]{1,0:T(8,128)(2,1)} %bitcast.34, bf16[128,512]{1,0:T(8,128)(2,1)} %get-tuple-element.10.write_ref, bf16[128,512]{1,0:T(8,128)(2,1)} %get-tuple-element.9.read_ref, f32[32,128]{1,0:T(8,128)} %bitcast.38, ...), custom_call_target="tpu_custom_call" | custom-call | tf_op jit(solution)/shard_map/pallas_call | solution.py:612
  125.0 1.9 %fusion = bf16[1,128,1024]{2,1,0:T(8,128)(2,1)} fusion(f32[128,1024]{1,0:T(8,128)} %get-tuple-element.8, bf16[128,1024]{1,0:T(8,128)(2,1)} %get-tuple-element.7), kind=kLoop, calls=%fused_computation.1 | loop fusion | flops 393216 | bytes 1048576 | tf_op jit(solution)/shard_map/broadcast_in_dim | solution.py:710

commit v4 on v3

--- a/solution.py
+++ b/solution.py
@@ -86,6 +86,8 @@
     hid_recv,
     ans_send,
     ans_recv,
+    half_in,
+    half_recv,
 ):
     n_ctx, n_seq, n_tp = sizes
     ctx, seq, tp = lax.axis_index("ctx"), lax.axis_index("seq"), lax.axis_index("tp")
@@ -306,11 +308,11 @@
     high_slots[...] = high.reshape(experts, capacity, tokens)
     low_slots[...] = low.reshape(experts, capacity, tokens)
 
-    @pl.loop(0, sources)
-    def _(r):
-        holder = flip(ctx, r % n_ctx, n_ctx) * n_seq + flip(seq, r // n_ctx, n_seq)
-        high_rows[r] = high_slots[holder // 2]
-        low_rows[r] = low_slots[holder // 2]
+    @pl.loop(0, experts)
+    def _(q):
+        holder = flip(ctx, q % n_ctx, n_ctx) * n_seq + flip(seq, q // n_ctx * 2, n_seq)
+        high_rows[q] = high_slots[holder // 2]
+        low_rows[q] = low_slots[holder // 2]
 
     fetches[0].wait()
 
@@ -429,22 +431,51 @@
             device_id_type=MESH,
         )
 
+    def near(r):
+        return (r // n_ctx) % 2 == 0
+
+    def slot(r):
+        return r // (2 * n_ctx) * n_ctx + r % n_ctx
+
+    def forward_copy(r):
+        return pltpu.make_async_remote_copy(
+            src_ref=received.at[r],
+            dst_ref=received.at[r + n_ctx],
+            send_sem=row_send.at[r + n_ctx],
+            recv_sem=row_recv.at[r + n_ctx],
+            device_id={"seq": flip(seq, 1, n_seq)},
+            device_id_type=MESH,
+        )
+
+    def half_copy(r):
+        return pltpu.make_async_remote_copy(
+            src_ref=answers.at[r],
+            dst_ref=half_in.at[slot(r - n_ctx)],
+            send_sem=ans_send.at[r],
+            recv_sem=half_recv.at[slot(r - n_ctx)],
+            device_id={"seq": flip(seq, 1, n_seq)},
+            device_id_type=MESH,
+        )
+
     def ans_copy(r):
         c, s = at_offset(r)
         return pltpu.make_async_remote_copy(
             src_ref=answers.at[r],
-            dst_ref=returned.at[r],
+            dst_ref=returned.at[slot(r)],
             send_sem=ans_send.at[r],
-            recv_sem=ans_recv.at[r],
+            recv_sem=ans_recv.at[slot(r)],
             device_id={"ctx": c, "seq": s},
             device_id_type=MESH,
         )
 
     @pl.loop(1, sources)
     def _(r):
-        row_copy(r).start()
+        @pl.when(near(r))
+        def _():
+            row_copy(r).start()
 
     received[0] = slots[(ctx * n_seq + seq) // 2]
+    forward_copy(0).start()
     fetches[1].wait()
     fetches[2].wait()
 
@@ -455,7 +486,7 @@
             for j in range(half_width // QB):
                 w_gate_up[rows, kind * half_width + j * QB : kind * half_width + (j + 1) * QB] = (
                     gate_up_ref[kind, rows, j * QB : (j + 1) * QB].astype(jnp.float32)
-                    * gate_up_scale_ref[kind, i, j]
+                    * gate_up_scale_ref[kind, pl.ds(i, 1), j : j + 1]
                 ).astype(jnp.bfloat16)
 
     @pl.loop(0, half_width // QB)
@@ -463,10 +494,12 @@
         rows = pl.ds(pl.multiple_of(i * QB, QB), QB)
         for j in range(feature_width // QB):
             w_down[rows, j * QB : (j + 1) * QB] = (
-                down_ref[rows, j * QB : (j + 1) * QB].astype(jnp.float32) * down_scale_ref[i, j]
+                down_ref[rows, j * QB : (j + 1) * QB].astype(jnp.float32) * down_scale_ref[pl.ds(i, 1), j : j + 1]
             ).astype(jnp.bfloat16)
 
-    @pl.loop(0, teams + 2)
+    delay = n_ctx // n_tp + 1
+
+    @pl.loop(0, teams + 3)
     def _(step):
         @pl.when(step < teams)
         def _():
@@ -480,6 +513,10 @@
                         row_copy(r).wait_recv()
                 else:
                     row_copy(r).wait_recv()
+
+                @pl.when(near(r) & (r > 0))
+                def _():
+                    forward_copy(r).start()
             rows = received[pl.ds(g * n_tp, n_tp)].reshape(n_tp * capacity, feature_width)
             both = jnp.dot(rows, w_gate_up[...], preferred_element_type=jnp.float32)
             partial_out[pl.ds(g * n_tp, n_tp)] = both.astype(jnp.bfloat16).reshape(
@@ -500,7 +537,7 @@
             for i in range(1, n_tp):
                 hid_copy(g, i).start()
 
-        @pl.when(step >= 2)
+        @pl.when((step >= 2) & (step < teams + 2))
         def _():
             g = step - 2
             for i in range(1, n_tp):
@@ -512,26 +549,41 @@
             )
             for i in range(n_tp):
                 r = g * n_tp + i
-                if i == 0:
-
-                    @pl.when(g > 0)
+
+                @pl.when((r // n_ctx) % 2 == 1)
+                def _():
+                    half_copy(r).start()
+
+        @pl.when(step >= 2 + delay)
+        def _():
+            for i in range(n_tp):
+                r = (step - 2 - delay) * n_tp + i
+
+                @pl.when(near(r))
+                def _():
+                    half_copy(r + n_ctx).wait_recv()
+                    answers[r] = (
+                        answers[r].astype(jnp.float32) + half_in[slot(r)].astype(jnp.float32)
+                    ).astype(jnp.bfloat16)
+
+                    @pl.when(r > 0)
                     def _():
                         ans_copy(r).start()
-                else:
-                    ans_copy(r).start()
 
     returned[0] = answers[0]
 
     @pl.loop(1, sources)
     def _(r):
-        ans_copy(r).wait_recv()
-
-    back = returned[...].reshape(sources * capacity, feature_width)
+        @pl.when(near(r))
+        def _():
+            ans_copy(r).wait_recv()
+
+    back = returned[...].reshape(experts * capacity, feature_width)
     contract = (((0,), (0,)), ((), ()))
     mixed = 0.0
     for rows in (high_rows, low_rows):
         mixed = mixed + lax.dot_general(
-            rows[...].reshape(sources * capacity, tokens),
+            rows[...].reshape(experts * capacity, tokens),
             back,
             contract,
             preferred_element_type=f32,
@@ -541,7 +593,14 @@
     @pl.loop(1, sources)
     def _(r):
         row_copy(r).wait_send()
-        ans_copy(r).wait_send()
+        pltpu.make_async_remote_copy(
+            src_ref=answers.at[r],
+            dst_ref=returned.at[0],
+            send_sem=ans_send.at[r],
+            recv_sem=ans_recv.at[0],
+            device_id={"seq": flip(seq, 1, n_seq)},
+            device_id_type=MESH,
+        ).wait_send()
 
     @pl.loop(0, teams)
     def _(g):
@@ -617,7 +676,7 @@
         ),
         in_specs=[vmem] * 6
         + [smem, vmem, hbm, vmem, vmem, vmem, vmem]
-        + [hbm, smem, hbm, smem],
+        + [hbm, vmem, hbm, vmem],
         out_specs=(vmem, vmem),
         scratch_shapes=[
             half(*out_weight.shape),
@@ -643,8 +702,8 @@
             dma((n_tp - 1,)),
             half(experts, capacity, tokens),
             half(experts, capacity, tokens),
-            half(sources, capacity, tokens),
-            half(sources, capacity, tokens),
+            half(experts, capacity, tokens),
+            half(experts, capacity, tokens),
             half(experts, capacity, features),
             half(features, 2 * half_width),
             half(half_width, features),
@@ -653,7 +712,7 @@
             half(shares, capacity, 2 * half_width),
             half(sources, capacity, half_width),
             half(sources, capacity, features),
-            half(sources, capacity, features),
+            half(experts, capacity, features),
             dma((sources,)),
             dma((sources,)),
             dma((shares,)),
@@ -661,7 +720,9 @@
             dma((shares,)),
             dma((shares,)),
             dma((sources,)),
-            dma((sources,)),
+            dma((experts,)),
+            half(experts, capacity, features),
+            dma((experts,)),
         ],
         compiler_params=pltpu.CompilerParams(
             collective_id=1, has_side_effects=True, vmem_limit_bytes=60 * 1024 * 1024

time: 127 us -> 125 us (0.984)
  Pallas kernels: 121 us -> 119 us
    pallas_call x1, Pallas kernels: 121 us -> 119 us  [both_layers(): pl.pallas_call(functools.partial(layer_kernel, sizes), out_shape=(jax.Sha...]
where the time goes in v4:
time: 125 us
  Pallas kernels  119 us (95%)
  local copies, waits for them, and re-layouts  4.32 us (3%)
  other arithmetic  1.87 us (1%)
    pallas_call x1, Pallas kernels, both_layers(): pl.pallas_call(functools.partial(layer_kernel, sizes), out_shape=(jax.Sha...  119 us

profile of v4, /device:TPU:19, one launch (start us, length us, event | category | flops | bytes accessed | tf_op | source)
XLA Modules:
  0.0 124.7 jit_solution(9747822027996020009)
XLA Ops:
  0.0 1.3 %copy.25 = f32[1,6,8]{2,1,0:T(8,128)} copy(f32[1,6,8]{2,0,1:T(1,128)} %param.33) | data formatting | bytes 384
  1.3 1.4 %copy.18.gate_up_scale_ref = f32[2,8,6]{2,1,0:T(8,128)} copy(f32[2,8,6]{1,0,2:T(2,128)} %bitcast.41) | data formatting | bytes 768 | tf_op jit(solution)/shard_map/squeeze | solution.py:786
  2.6 1.7 %copy_bitcast_fusion = (bf16[128,512]{1,0:T(8,128)(2,1)}, bf16[128,512]{1,0:T(8,128)(2,1)}) fusion(bf16[16,8,4,128]{3,2,1,0:T(4,128)(2,1)} %bitcast.36, bf16[16,8,4,128]{3,2,1,0:T(4,128)(2,1)} %bitcast.37), kind=kLoop, calls=%fused_computation.2 | loop fusion | bytes 524288 | tf_op jit(solution)/shard_map/reshape;squeeze | solution.py:734
  4.3 118.5 %shard_map.163 = (bf16[128,1024]{1,0:T(8,128)(2,1)}, f32[128,1024]{1,0:T(8,128)}) custom-call(bf16[128,2048]{1,0:T(8,128)(2,1)} %bitcast.33, bf16[128,2048]{1,0:T(8,128)(2,1)} %bitcast.34, bf16[128,512]{1,0:T(8,128)(2,1)} %get-tuple-element.10.write_ref, bf16[128,512]{1,0:T(8,128)(2,1)} %get-tuple-element.9.read_ref, f32[32,128]{1,0:T(8,128)} %bitcast.38, ...), custom_call_target="tpu_custom_call" | custom-call | tf_op jit(solution)/shard_map/pallas_call | solution.py:671
  122.9 1.9 %fusion = bf16[1,128,1024]{2,1,0:T(8,128)(2,1)} fusion(f32[128,1024]{1,0:T(8,128)} %get-tuple-element.8, bf16[128,1024]{1,0:T(8,128)(2,1)} %get-tuple-element.7), kind=kLoop, calls=%fused_computation.1 | loop fusion | flops 393216 | bytes 1048576 | tf_op jit(solution)/shard_map/broadcast_in_dim | solution.py:771

commit v5 on v4

--- a/solution.py
+++ b/solution.py
@@ -314,7 +314,30 @@
         high_rows[q] = high_slots[holder // 2]
         low_rows[q] = low_slots[holder // 2]
 
-    fetches[0].wait()
+    for fetch in fetches:
+        fetch.wait()
+
+    def scale_gate_up(i):
+        rows = slice(i * QB, (i + 1) * QB)
+        for kind in range(2):
+            for j in range(half_width // QB):
+                lanes = slice(j * QB, (j + 1) * QB)
+                target = slice(kind * half_width + j * QB, kind * half_width + (j + 1) * QB)
+                w_gate_up[rows, target] = (
+                    gate_up_ref[kind, rows, lanes].astype(f32)
+                    * gate_up_scale_ref[j, kind : kind + 1, i : i + 1]
+                ).astype(bf16)
+
+    def scale_down(i):
+        rows = slice(i * QB, (i + 1) * QB)
+        for j in range(feature_width // QB):
+            lanes = slice(j * QB, (j + 1) * QB)
+            w_down[rows, lanes] = (
+                down_ref[rows, lanes].astype(f32) * down_scale_ref[i, :, j : j + 1]
+            ).astype(bf16)
+
+    chores = [functools.partial(scale_gate_up, i) for i in range(feature_width // QB)]
+    chores += [functools.partial(scale_down, i) for i in range(half_width // QB)]
 
     def multiply(g):
         for a in range(1, n_ctx, 2):
@@ -335,6 +358,8 @@
         for a in range(2, n_ctx, 2):
             rows_copy(g, 0, a, a).wait_recv()
             rows_copy(g, a, a + 1, 1).start()
+        for chore in chores[g::groups]:
+            chore()
         if g > 0:
             multiply(g - 1)
     multiply(groups - 1)
@@ -476,26 +501,6 @@
 
     received[0] = slots[(ctx * n_seq + seq) // 2]
     forward_copy(0).start()
-    fetches[1].wait()
-    fetches[2].wait()
-
-    @pl.loop(0, feature_width // QB)
-    def _(i):
-        rows = pl.ds(pl.multiple_of(i * QB, QB), QB)
-        for kind in range(2):
-            for j in range(half_width // QB):
-                w_gate_up[rows, kind * half_width + j * QB : kind * half_width + (j + 1) * QB] = (
-                    gate_up_ref[kind, rows, j * QB : (j + 1) * QB].astype(jnp.float32)
-                    * gate_up_scale_ref[kind, pl.ds(i, 1), j : j + 1]
-                ).astype(jnp.bfloat16)
-
-    @pl.loop(0, half_width // QB)
-    def _(i):
-        rows = pl.ds(pl.multiple_of(i * QB, QB), QB)
-        for j in range(feature_width // QB):
-            w_down[rows, j * QB : (j + 1) * QB] = (
-                down_ref[rows, j * QB : (j + 1) * QB].astype(jnp.float32) * down_scale_ref[pl.ds(i, 1), j : j + 1]
-            ).astype(jnp.bfloat16)
 
     delay = n_ctx // n_tp + 1
 
@@ -742,9 +747,9 @@
         routes.T,
         route_weight.T,
         gate_up,
-        gate_up_scale,
+        jnp.transpose(gate_up_scale, (2, 0, 1)),
         down,
-        down_scale,
+        down_scale[:, None, :],
     )
     return (stream.astype(jnp.float32) + mixed).astype(jnp.bfloat16)
 

time: 125 us -> 122 us (0.976)
  local copies, waits for them, and re-layouts: 4.32 us -> 1.69 us
    squeeze x1 -> x0, local copies, waits for them, and re-layouts: 1.37 us -> none  [on_device(): gate_up_scales[0]]
    unnamed x1 -> x0, local copies, waits for them, and re-layouts: 1.27 us -> none
where the time goes in v5:
time: 122 us; the launch traced here: 121 us
  Pallas kernels  118 us (97%)
  other arithmetic  1.87 us (2%)
  local copies, waits for them, and re-layouts  1.69 us (1%)
    pallas_call x1, Pallas kernels, both_layers(): pl.pallas_call(functools.partial(layer_kernel, sizes), out_shape=(jax.Sha...  118 us

profile of v5, /device:TPU:19, one launch (start us, length us, event | category | flops | bytes accessed | tf_op | source)
XLA Modules:
  0.0 121.5 jit_solution(15451526766310818275)
XLA Ops:
  0.0 1.7 %copy_bitcast_fusion = (bf16[128,512]{1,0:T(8,128)(2,1)}, bf16[128,512]{1,0:T(8,128)(2,1)}) fusion(bf16[16,8,4,128]{3,2,1,0:T(4,128)(2,1)} %bitcast.36, bf16[16,8,4,128]{3,2,1,0:T(4,128)(2,1)} %bitcast.37), kind=kLoop, calls=%fused_computation.2 | loop fusion | bytes 524288 | tf_op jit(solution)/shard_map/reshape;squeeze | solution.py:739
  1.7 117.9 %shard_map.163 = (bf16[128,1024]{1,0:T(8,128)(2,1)}, f32[128,1024]{1,0:T(8,128)}) custom-call(bf16[128,2048]{1,0:T(8,128)(2,1)} %bitcast.33, bf16[128,2048]{1,0:T(8,128)(2,1)} %bitcast.34, bf16[128,512]{1,0:T(8,128)(2,1)} %get-tuple-element.10.write_ref, bf16[128,512]{1,0:T(8,128)(2,1)} %get-tuple-element.9.read_ref, f32[32,128]{1,0:T(8,128)} %bitcast.38, ...), custom_call_target="tpu_custom_call" | custom-call | tf_op jit(solution)/shard_map/pallas_call | solution.py:676
  119.6 1.9 %fusion = bf16[1,128,1024]{2,1,0:T(8,128)(2,1)} fusion(f32[128,1024]{1,0:T(8,128)} %get-tuple-element.8, bf16[128,1024]{1,0:T(8,128)(2,1)} %get-tuple-element.7), kind=kLoop, calls=%fused_computation.1 | loop fusion | flops 393216 | bytes 1048576 | tf_op jit(solution)/shard_map/broadcast_in_dim | solution.py:776
